TPU v7x, 256 devices: a whole 4x4x8 slice. The times are simulated.
256 devices in a mesh: cells: 64 (over z, x, core), chan: 4 (over y).
Axes of the slice: x: 4, y: 4, z: 8, core: 2. Of those that a mesh axis runs over, the one named last changes fastest.
Arguments:
- charges: bfloat16 [128, 65536], P('chan', 'cells'), may hold values from -6 to 6
- basis: float32 [25, 65536], P(None, 'cells'), may hold values from -1.5 to 1.5
- atom_leaf: int32 [65536], P('cells'), may hold values from 0 to 8191, as said below
- leaf_lists: int32 [64, 8192], P(None, 'cells'), may hold values from -1 to 8191, as said below
- coarse_lists: int32 [64, 1024], P(None, 'cells'), may hold values from -1 to 1023, as said below
- up_ops: bfloat16 [8, 25, 25], replicated, may hold values from -0.4375 to 0.4375
- down_ops: bfloat16 [8, 25, 25], replicated, may hold values from -1.25 to 1.25
- leaf_ops: bfloat16 [25, 25, 64], replicated, may hold values from -0.15625 to 0.15625
- coarse_ops: bfloat16 [25, 25, 64], replicated, may hold values from -0.15625 to 0.15625
- mix: bfloat16 [128, 128], replicated, may hold values from -0.5 to 0.5
- cotangent: bfloat16 [128, 65536], P('chan', 'cells'), may hold values from -0.005859375 to 0.005859375
Outputs:
- refined: bfloat16 [128, 65536], P('chan', 'cells')
- grad_leaf_ops: float32 [25, 25, 64], replicated
- grad_coarse_ops: float32 [25, 25, 64], replicated
Inputs may be any that keep to these rules, and one draw needn't show every extreme that they name: `atom_leaf`: an atom's leaf is one of the 128 consecutive leaves whose block along cells holds that atom. `leaf_lists`: entry [s, t] is -1 for an empty slot, else a leaf within 64 leaves of the block of 128 leaves that holds t. `coarse_lists`: entry [s, p] is -1 for an empty slot, else a parent cell within 8 cells of the block of 16 parent cells that holds p.
All inputs are finite; a program needn't handle non-finite values.
Results may differ from a plain program's by a relative error of at most 0.014.
Values may be sent and summed in bfloat16 or wider, within the bound.
A program may use at most 128 MiB of HBM per device.

v0:
```python
import jax
import jax.numpy as jnp
from jax import lax
from jax.sharding import PartitionSpec as P

SLOT_BLOCK = 16


def extended(block, sides, width):
    for axis, dim in sides:
        count = lax.axis_size(axis)
        forward = [(i, i + 1) for i in range(count - 1)]
        backward = [(target, source) for source, target in forward]
        low = lax.ppermute(
            lax.slice_in_dim(block, block.shape[dim] - width, None, axis=dim), axis, forward
        )
        high = lax.ppermute(lax.slice_in_dim(block, 0, width, axis=dim), axis, backward)
        block = jnp.concatenate([low, block, high], axis=dim)
    return block


def spread(weights, values, local_leaf, leaf_dev):
    kcount, atoms = weights.shape
    chan_part = values.shape[0]
    width = min(1024, atoms)

    def spread_accumulate(counter, running):
        member = (local_leaf[:, None] == jnp.arange(leaf_dev, dtype=jnp.int32)[None, :]).astype(
            jnp.bfloat16
        )
        scaled = (weights[:, None, :] * values[None].astype(jnp.float32)).astype(jnp.bfloat16)
        return running + jnp.dot(
            scaled.reshape(kcount * chan_part, width), member, preferred_element_type=jnp.float32
        )

    start_value = jnp.zeros((kcount * chan_part, leaf_dev), jnp.float32)
    result = lax.fori_loop(0, atoms // width, spread_accumulate, start_value)
    return result.reshape(kcount, chan_part, leaf_dev)


def collect(weights, fields, local_leaf):
    kcount, chan_part, leaf_dev = fields.shape
    atoms = weights.shape[1]
    width = min(1024, atoms)
    flat_fields = fields.reshape(kcount * chan_part, leaf_dev)

    def collect_accumulate(counter, running):
        member = (jnp.arange(leaf_dev, dtype=jnp.int32)[:, None] == local_leaf[None, :]).astype(
            jnp.bfloat16
        )
        per_atom = jnp.dot(flat_fields, member, preferred_element_type=jnp.float32).reshape(
            kcount, chan_part, width
        )
        summed = jnp.sum(weights[:, None, :] * per_atom, axis=0)
        return summed

    start_value = jnp.zeros((chan_part, atoms), jnp.float32)
    return lax.fori_loop(0, atoms // width, collect_accumulate, start_value)


def pick(source, group_list, first_cell):
    valid = group_list >= 0
    position = jnp.where(valid, group_list - first_cell, 0)
    picked = jnp.take(source, position, axis=2)
    return picked * valid.astype(jnp.bfloat16)[None, None]


def translate(source, lists, first_cell, ops):
    kcount, chan_part, _ = source.shape
    slot_count, targets = lists.shape
    groups = slot_count // SLOT_BLOCK
    list_groups = lists.reshape(groups, SLOT_BLOCK, targets)
    op_groups = jnp.transpose(ops.reshape(kcount, kcount, groups, SLOT_BLOCK), (2, 3, 0, 1))

    def translate_advance(running, pieces):
        group_list, group_ops = pieces
        picked = pick(source, group_list, first_cell)
        return (
            running
            + jnp.einsum("okj,jcot->kct", group_ops, picked, preferred_element_type=jnp.float32),
            None,
        )

    start_value = jnp.zeros((kcount, chan_part, targets), jnp.float32)
    result, _ = lax.scan(translate_advance, start_value, (list_groups, op_groups))
    return result


def slot_gradients(source, lists, first_cell, fields):
    kcount = source.shape[0]
    slot_count, targets = lists.shape
    groups = slot_count // SLOT_BLOCK
    list_groups = lists.reshape(groups, SLOT_BLOCK, targets)

    def slot_advance(carried, group_list):
        picked = pick(source, group_list, first_cell)
        return (
            carried,
            jnp.einsum("kct,jcot->kjo", fields, picked, preferred_element_type=jnp.float32),
        )

    _, stacked = lax.scan(slot_advance, jnp.zeros((), jnp.float32), list_groups)
    return jnp.transpose(stacked, (1, 2, 0, 3)).reshape(kcount, kcount, slot_count)


def local(
    charges,
    basis,
    atom_leaf,
    leaf_lists,
    coarse_lists,
    up_ops,
    down_ops,
    leaf_ops,
    coarse_ops,
    mix,
    cotangent,
):
    chan_part = charges.shape[0]
    kcount = basis.shape[0]
    leaf_dev = leaf_lists.shape[1]
    coarse_dev = coarse_lists.shape[1]
    cells_pos = lax.axis_index("cells")
    chan_pos = lax.axis_index("chan")
    local_leaf = atom_leaf - cells_pos * leaf_dev
    moments = spread(basis, charges, local_leaf, leaf_dev).astype(jnp.bfloat16)
    grouped = moments.reshape(kcount, chan_part, coarse_dev, 8)
    coarse = jnp.einsum(
        "okj,jcpo->kcp", up_ops, grouped, preferred_element_type=jnp.float32
    ).astype(jnp.bfloat16)
    leaf_source = extended(moments, (("cells", 2),), leaf_dev // 2)
    leaf_first = cells_pos * leaf_dev - leaf_dev // 2
    coarse_source = extended(coarse, (("cells", 2),), coarse_dev // 2)
    coarse_first = cells_pos * coarse_dev - coarse_dev // 2
    near_field = translate(leaf_source, leaf_lists, leaf_first, leaf_ops)
    far_field = translate(coarse_source, coarse_lists, coarse_first, coarse_ops).astype(
        jnp.bfloat16
    )
    child = jnp.einsum("okj,jcp->kcpo", down_ops, far_field, preferred_element_type=jnp.float32)
    expansion = (near_field + child.reshape(kcount, chan_part, leaf_dev)).astype(jnp.bfloat16)
    potential = collect(basis, expansion, local_leaf).astype(jnp.bfloat16)
    rows_mine = lax.dynamic_slice_in_dim(mix, chan_pos * chan_part, chan_part, 0)
    cols_mine = lax.dynamic_slice_in_dim(mix, chan_pos * chan_part, chan_part, 1)
    mixed = lax.dot_general(
        cols_mine,
        lax.all_gather(potential, "chan", axis=0, tiled=True),
        (((0,), (0,)), ((), ())),
        preferred_element_type=jnp.float32,
    )
    back_sum = jnp.dot(
        rows_mine,
        lax.all_gather(cotangent, "chan", axis=0, tiled=True),
        preferred_element_type=jnp.float32,
    )
    refined = (charges.astype(jnp.float32) + mixed).astype(jnp.bfloat16)
    back_potential = back_sum.astype(jnp.bfloat16)
    back_expansion = spread(basis, back_potential, local_leaf, leaf_dev).astype(jnp.bfloat16)
    back_grouped = back_expansion.reshape(kcount, chan_part, coarse_dev, 8)
    back_far = jnp.einsum(
        "okj,kcpo->jcp", down_ops, back_grouped, preferred_element_type=jnp.float32
    ).astype(jnp.bfloat16)
    grad_leaf = slot_gradients(leaf_source, leaf_lists, leaf_first, back_expansion)
    grad_coarse = slot_gradients(coarse_source, coarse_lists, coarse_first, back_far)
    grad_leaf, grad_coarse = lax.psum((grad_leaf, grad_coarse), ("cells", "chan"))
    return (refined, grad_leaf, grad_coarse)


def solution(mesh):
    placed = (
        P("chan", "cells"),
        P(None, "cells"),
        P("cells"),
        P(None, "cells"),
        P(None, "cells"),
        P(),
        P(),
        P(),
        P(),
        P(),
        P("chan", "cells"),
    )
    return jax.shard_map(
        local, mesh=mesh, in_specs=placed, out_specs=(P("chan", "cells"), P(), P()), check_vma=False
    )
```

profile of v0, /device:TPU:1, one launch (start us, length us, event | category | flops | bytes accessed | tf_op | source)
XLA Modules:
  0.0 722.5 jit_solution(9109661945923828574)
XLA Ops:
  8.8 1.6 fusion.47
  11.2 5.1 collective-permute-start.1
  16.4 1.9 collective-permute-start
  18.3 1.7 copy.72
  20.4 3.1 collective-permute-start.3
  23.5 2.5 collective-permute-start.2
  26.0 9.4 %all_gather.7 = bf16[128,1024]{1,0:T(8,128)(2,1)S(1)} all-gather(bf16[32,1024]{1,0:T(8,128)(2,1)S(1)} %copy-done.9), channel_id=1, replica_groups=mesh['cells'=64,'chan'=4] {'chan'}, dimensions={0}, use_global_device_ids=true | all-gather | bytes 327680 | tf_op jit(solution)/shard_map/all_gather | solution.py:152
  36.3 1.7 copy.75
  39.2 1.7 copy.40
  43.1 13.1 %while.57 = (s32[]{:T(128)}, f32[25,32,16]{1,0,2:T(8,128)S(1)}, bf16[4,16,25,25]{3,2,1,0:T(8,128)(2,1)S(1)}, s32[4,16,16]{2,1,0:T(8,128)S(1)}, s32[]{:T(128)}, /...) while((s32[]{:T(128)}, f32[25,32,16]{1,0,2:T(8,128)S(1)}, ...), condition=%wide.region_3.6_spmd.clone, body=%wide.region_2.5_spmd.clone.sunk | while | flops 10678787 | bytes 4553847 | solution.py:85
  56.3 17.5 %while.15 = (s32[]{:T(128)}, f32[4,25,25,16]{1,2,3,0:T(8,128)}, s32[4,16,16]{2,1,0:T(8,128)S(1)}, s32[]{:T(128)}, bf16[25,32,32]{1,0,2:T(8,128)(2,1)S(1)}, /*index=5*/bf16[25,32,16]{1,0,2:T(8,128)(2,1)}, s32[]{:T(128)}) while((s32[]{:T(128)}, f32[4,25,25,16]{1,2,3,0:T(8,128)}, s32[4,16,16]{2,1,0:T(8,128)S(1)}, s32[]{:T(128)}, ...), condition=%wide.region_9.12_spmd, body=%wide.region_8.11_spmd.sunk | while | flops 10653186 | bytes 3270785 | solution.py:102
  59.0 1.7 fusion.96
  63.3 1.7 fusion.96
  67.7 1.7 fusion.96
  72.1 1.7 fusion.96
  75.6 2.9 copy.61
  79.8 3.0 copy.41
  82.8 193.7 %while.56 = (s32[]{:T(128)}, f32[25,32,128]{2,0,1:T(8,128)}, bf16[4,16,25,25]{3,2,1,0:T(8,128)(2,1)}, s32[4,16,128]{2,1,0:T(8,128)S(1)}, s32[]{:T(128)}, /*index...) while((s32[]{:T(128)}, f32[25,32,128]{2,0,1:T(8,128)}, bf16[4,16,25,25]{3,2,1,0:T(8,128)(2,1)}, ...), condition=%wide.region_1.3_spmd.clone, body=%wide.region_0.2_spmd.clone.sunk | while | flops 90349568 | bytes 18425984 | solution.py:85
  82.9 19.3 %gather_fusion.2 = bf16[2048,25,32]{2,1,0:T(8,128)(2,1)} fusion(bf16[25,32,256]{1,0,2:T(8,128)(2,1)S(1)} %get-tuple-element.527, s32[2048]{0:T(1024)S(1)} %bitcast_clamp_fusion.5), kind=kCustom, calls=%fused_computation.clone.clone.1 | custom fusion | bytes 6561792 | tf_op jit(solution)/shard_map/while/body/eval_jaxpr/jit(_take)/gather | solution.py:64
  102.2 24.5 %copy.113 = bf16[16,128,25,32]{1,2,0,3:T(8,128)(2,1)} copy(bf16[16,128,25,32]{3,2,1,0:T(8,128)(2,1)} %bitcast.208) | data formatting | bytes 6553600 | tf_op jit(solution)/shard_map/while/body/eval_jaxpr/jit(_take)/gather | solution.py:64
  126.7 4.5 fusion.98
  131.2 19.3 %gather_fusion.2 = bf16[2048,25,32]{2,1,0:T(8,128)(2,1)} fusion(bf16[25,32,256]{1,0,2:T(8,128)(2,1)S(1)} %get-tuple-element.527, s32[2048]{0:T(1024)S(1)} %bitcast_clamp_fusion.5), kind=kCustom, calls=%fused_computation.clone.clone.1 | custom fusion | bytes 6561792 | tf_op jit(solution)/shard_map/while/body/eval_jaxpr/jit(_take)/gather | solution.py:64
  150.5 24.5 %copy.113 = bf16[16,128,25,32]{1,2,0,3:T(8,128)(2,1)} copy(bf16[16,128,25,32]{3,2,1,0:T(8,128)(2,1)} %bitcast.208) | data formatting | bytes 6553600 | tf_op jit(solution)/shard_map/while/body/eval_jaxpr/jit(_take)/gather | solution.py:64
  175.0 4.6 fusion.98
  179.6 19.3 %gather_fusion.2 = bf16[2048,25,32]{2,1,0:T(8,128)(2,1)} fusion(bf16[25,32,256]{1,0,2:T(8,128)(2,1)S(1)} %get-tuple-element.527, s32[2048]{0:T(1024)S(1)} %bitcast_clamp_fusion.5), kind=kCustom, calls=%fused_computation.clone.clone.1 | custom fusion | bytes 6561792 | tf_op jit(solution)/shard_map/while/body/eval_jaxpr/jit(_take)/gather | solution.py:64
  198.9 24.5 %copy.113 = bf16[16,128,25,32]{1,2,0,3:T(8,128)(2,1)} copy(bf16[16,128,25,32]{3,2,1,0:T(8,128)(2,1)} %bitcast.208) | data formatting | bytes 6553600 | tf_op jit(solution)/shard_map/while/body/eval_jaxpr/jit(_take)/gather | solution.py:64
  223.5 4.6 fusion.98
  228.1 19.3 %gather_fusion.2 = bf16[2048,25,32]{2,1,0:T(8,128)(2,1)} fusion(bf16[25,32,256]{1,0,2:T(8,128)(2,1)S(1)} %get-tuple-element.527, s32[2048]{0:T(1024)S(1)} %bitcast_clamp_fusion.5), kind=kCustom, calls=%fused_computation.clone.clone.1 | custom fusion | bytes 6561792 | tf_op jit(solution)/shard_map/while/body/eval_jaxpr/jit(_take)/gather | solution.py:64
  247.4 24.5 %copy.113 = bf16[16,128,25,32]{1,2,0,3:T(8,128)(2,1)} copy(bf16[16,128,25,32]{3,2,1,0:T(8,128)(2,1)} %bitcast.208) | data formatting | bytes 6553600 | tf_op jit(solution)/shard_map/while/body/eval_jaxpr/jit(_take)/gather | solution.py:64
  271.9 4.6 fusion.98
  278.3 9.4 %all_gather.6 = bf16[128,1024]{1,0:T(8,128)(2,1)S(1)} all-gather(bf16[32,1024]{1,0:T(8,128)(2,1)S(1)} %multiply_reduce_fusion), channel_id=1, replica_groups=mesh['cells'=64,'chan'=4] {'chan'}, dimensions={0}, use_global_device_ids=true | all-gather | bytes 327680 | tf_op jit(solution)/shard_map/all_gather | solution.py:146
  287.7 151.2 %while.14 = (s32[]{:T(128)}, f32[4,25,25,16]{1,3,2,0:T(8,128)}, s32[4,16,128]{2,1,0:T(8,128)S(1)}, s32[]{:T(128)}, bf16[25,32,256]{1,0,2:T(8,128)(2,1)S(1)}, /*index=5*/bf16[25,32,128]{2,0,1:T(8,128)(2,1)S(1)}, s32[]{:T(128)}) while((s32[]{:T(128)}, f32[4,25,25,16]{1,3,2,0:T(8,128)}, s32[4,16,128]{2,1,0:T(8,128)S(1)}, s32[]{:T(128)}, ...), condition=%wide.region_6.9_spmd, body=%wide.region_5.8_spmd.sunk | while | flops 85229568 | bytes 16853100 | solution.py:102
  287.7 19.3 %gather_fusion = bf16[2048,25,32]{2,1,0:T(8,128)(2,1)} fusion(bf16[25,32,256]{1,0,2:T(8,128)(2,1)S(1)} %get-tuple-element.572, s32[2048]{0:T(1024)S(1)} %bitcast_clamp_fusion.4), kind=kCustom, calls=%fused_computation.2.clone.clone.1 | custom fusion | bytes 6561792 | tf_op jit(solution)/shard_map/while/body/eval_jaxpr/jit(_take)/gather | solution.py:64
  307.0 14.9 %copy.110 = bf16[16,128,25,32]{1,0,3,2:T(8,128)(2,1)} copy(bf16[16,128,25,32]{3,2,1,0:T(8,128)(2,1)} %bitcast.209) | data formatting | bytes 6553600 | tf_op jit(solution)/shard_map/while/body/eval_jaxpr/jit(_take)/gather | solution.py:64
  321.9 3.6 fusion.93
  325.5 19.3 %gather_fusion = bf16[2048,25,32]{2,1,0:T(8,128)(2,1)} fusion(bf16[25,32,256]{1,0,2:T(8,128)(2,1)S(1)} %get-tuple-element.572, s32[2048]{0:T(1024)S(1)} %bitcast_clamp_fusion.4), kind=kCustom, calls=%fused_computation.2.clone.clone.1 | custom fusion | bytes 6561792 | tf_op jit(solution)/shard_map/while/body/eval_jaxpr/jit(_take)/gather | solution.py:64
  344.8 14.9 %copy.110 = bf16[16,128,25,32]{1,0,3,2:T(8,128)(2,1)} copy(bf16[16,128,25,32]{3,2,1,0:T(8,128)(2,1)} %bitcast.209) | data formatting | bytes 6553600 | tf_op jit(solution)/shard_map/while/body/eval_jaxpr/jit(_take)/gather | solution.py:64
  359.7 3.6 fusion.93
  363.3 19.3 %gather_fusion = bf16[2048,25,32]{2,1,0:T(8,128)(2,1)} fusion(bf16[25,32,256]{1,0,2:T(8,128)(2,1)S(1)} %get-tuple-element.572, s32[2048]{0:T(1024)S(1)} %bitcast_clamp_fusion.4), kind=kCustom, calls=%fused_computation.2.clone.clone.1 | custom fusion | bytes 6561792 | tf_op jit(solution)/shard_map/while/body/eval_jaxpr/jit(_take)/gather | solution.py:64
  382.6 14.9 %copy.110 = bf16[16,128,25,32]{1,0,3,2:T(8,128)(2,1)} copy(bf16[16,128,25,32]{3,2,1,0:T(8,128)(2,1)} %bitcast.209) | data formatting | bytes 6553600 | tf_op jit(solution)/shard_map/while/body/eval_jaxpr/jit(_take)/gather | solution.py:64
  397.5 3.6 fusion.93
  401.1 19.3 %gather_fusion = bf16[2048,25,32]{2,1,0:T(8,128)(2,1)} fusion(bf16[25,32,256]{1,0,2:T(8,128)(2,1)S(1)} %get-tuple-element.572, s32[2048]{0:T(1024)S(1)} %bitcast_clamp_fusion.4), kind=kCustom, calls=%fused_computation.2.clone.clone.1 | custom fusion | bytes 6561792 | tf_op jit(solution)/shard_map/while/body/eval_jaxpr/jit(_take)/gather | solution.py:64
  420.4 14.9 %copy.110 = bf16[16,128,25,32]{1,0,3,2:T(8,128)(2,1)} copy(bf16[16,128,25,32]{3,2,1,0:T(8,128)(2,1)} %bitcast.209) | data formatting | bytes 6553600 | tf_op jit(solution)/shard_map/while/body/eval_jaxpr/jit(_take)/gather | solution.py:64
  435.2 3.6 fusion.93
  438.8 2.9 copy.54
  442.7 268.5 %all-reduce.3.cloned.1.call-done = (f32[25,25,64]{1,2,0:T(8,128)}, f32[25,25,64]{1,2,0:T(8,128)}) async-done(((f32[25,25,64]{1,2,0:T(8,128)}, f32[25,25,64]{1,2,0:T(8,128)}), (f32[25,25,64]{1,2,0:T(8,128)}, f32[25,25,64]{1,2,0:T(8,128)})) %all-reduce.3.cloned.1.call-update) | async-done | bytes 320016 | tf_op jit(solution)/shard_map/psum | solution.py:164
  711.2 2.2 copy.62
  713.5 2.2 copy.63
  (146 shorter events, 36.5 us)
Async XLA Ops:
  7.2 28.2 %copy-start = (bf16[128,128]{1,0:T(8,128)(2,1)S(1)}, bf16[128,128]{1,0:T(8,128)(2,1)}, u32[]{:S(2)}) copy-start(bf16[128,128]{1,0:T(8,128)(2,1)} %param.32) | copy-start | bytes 98308
  7.2 704.1 %all-reduce.3.cloned.1.call-start = ((), (), s32[]{:S(2)}) async-start(), calls=%async_computation | async-start | bytes 3276800 | tf_op jit(solution)/shard_map/psum | solution.py:164
  8.1 11.9 %copy-start.7 = (bf16[8,25,25]{2,0,1:T(8,128)(2,1)S(1)}, bf16[8,25,25]{2,0,1:T(8,128)(2,1)}, u32[]{:S(2)}) copy-start(bf16[8,25,25]{2,0,1:T(8,128)(2,1)} %param.28) | copy-start | bytes 30004
  10.4 15.6 %copy-start.9 = (bf16[32,1024]{1,0:T(8,128)(2,1)S(1)}, bf16[32,1024]{1,0:T(8,128)(2,1)}, u32[]{:S(2)}) copy-start(bf16[32,1024]{1,0:T(8,128)(2,1)} %param.33) | copy-start | bytes 196612
  10.4 25.1 %copy-start.11 = (f32[25,1024]{1,0:T(8,128)S(1)}, f32[25,1024]{1,0:T(8,128)}, u32[]{:S(2)}) copy-start(f32[25,1024]{1,0:T(8,128)} %param.24) | copy-start | bytes 307204
  11.2 67.3 %collective-permute-start.1 = (bf16[25,32,64]{2,1,0:T(8,128)(2,1)}, bf16[25,32,64]{2,1,0:T(8,128)(2,1)}, u32[]{:S(2)}, u32[]{:S(2)}) collective-permute-start(bf16[25,32,64]{2,1,0:T(8,128)(2,1)} %get-tuple-element.331), channel_id=1, source_target_pairs={{4,0},{8,4},{12,8},{16,12},{20,16},{24,20},{28,24},{32,28},{36,32}... | collective-permute-start | bytes 307208 | tf_op jit(solution)/shard_map/ppermute | solution.py:17
  16.4 62.2 %collective-permute-start = (bf16[25,32,64]{2,1,0:T(8,128)(2,1)}, bf16[25,32,64]{2,1,0:T(8,128)(2,1)}, u32[]{:S(2)}, u32[]{:S(2)}) collective-permute-start(bf16[25,32,64]{2,1,0:T(8,128)(2,1)} %get-tuple-element.330), channel_id=1, source_target_pairs={{0,4},{4,8},{8,12},{12,16},{16,20},{20,24},{24,28},{28,32},{32,36}... | collective-permute-start | bytes 307208 | tf_op jit(solution)/shard_map/ppermute | solution.py:14
  20.4 17.6 %copy-start.8 = (bf16[8,25,25]{2,0,1:T(8,128)(2,1)S(1)}, bf16[8,25,25]{2,0,1:T(8,128)(2,1)}, u32[]{:S(2)}) copy-start(bf16[8,25,25]{2,0,1:T(8,128)(2,1)} %param.29) | copy-start | bytes 30004
  20.4 22.3 %collective-permute-start.3 = (bf16[25,32,8]{0,1,2:T(8,128)(2,1)S(1)}, bf16[25,32,8]{0,1,2:T(8,128)(2,1)S(1)}, u32[]{:S(2)}, u32[]{:S(2)}) collective-permute-start(bf16[25,32,8]{0,1,2:T(8,128)(2,1)S(1)} %get-tuple-element.333), channel_id=1, source_target_pairs={{4,0},{8,4},{12,8},{16,12},{20,16},{24,20},{28,24},{32,28},{36,32}... | collective-permute-start | bytes 38408 | tf_op jit(solution)/shard_map/ppermute | solution.py:17
  23.5 19.2 %collective-permute-start.2 = (bf16[25,32,8]{0,1,2:T(8,128)(2,1)S(1)}, bf16[25,32,8]{0,1,2:T(8,128)(2,1)S(1)}, u32[]{:S(2)}, u32[]{:S(2)}) collective-permute-start(bf16[25,32,8]{0,1,2:T(8,128)(2,1)S(1)} %get-tuple-element.332), channel_id=1, source_target_pairs={{0,4},{4,8},{8,12},{12,16},{16,20},{20,24},{24,28},{28,32},{32,36}... | collective-permute-start | bytes 38408 | tf_op jit(solution)/shard_map/ppermute | solution.py:14
  35.6 3.6 copy-start.4
  36.3 4.6 copy-start.5
  36.3 5.5 copy-start.10
  58.1 0.9 copy-start.6
  62.4 0.9 copy-start.6
  66.8 0.9 copy-start.6
  71.2 0.9 copy-start.6
  78.5 4.3 copy-start.1
  82.8 194.9 %copy-start.12 = (f32[25,1024]{1,0:T(8,128)S(1)}, f32[25,1024]{1,0:T(8,128)}, u32[]{:S(2)}) copy-start(f32[25,1024]{1,0:T(8,128)} %param.24) | copy-start | bytes 307204
  276.5 11.2 %copy-start.2 = (bf16[25,32,128]{2,0,1:T(8,128)(2,1)S(1)}, bf16[25,32,128]{2,0,1:T(8,128)(2,1)}, u32[]{:S(2)}) copy-start(bf16[25,32,128]{2,0,1:T(8,128)(2,1)} %copy.53) | copy-start | bytes 614404
  438.8 2.9 copy-start.3
Sparse Core Ops, SparseCore 0:
  441.9 269.3 all-reduce.2
where the time goes:
time: 726 us; the launch traced here: 723 us
  local copies, waits for them, and re-layouts  352 us (48%)
  waiting for transfers between devices  269 us (37%)
  matrix products  49.3 us (7%)
  blocking collectives  18.7 us (3%)
  between operations  14.3 us (2%)
  starting transfers between devices  12.6 us (2%)
    gather x32, local copies, waits for them, and re-layouts, pick(): picked = jnp.take(source, position, axis=2)  325 us
    psum x1, waiting for transfers between devices, local(): lax.psum((grad_leaf, grad_coarse), ('cells', 'chan'))  269 us
    dot_general x8, matrix products, translate_advance(): jnp.einsum('okj,jcot->kct', group_ops, picked, preferred_element_type=jnp...  22.9 us
    dot_general x8, matrix products, slot_advance(): jnp.einsum('kct,jcot->kjo', fields, picked, preferred_element_type=jnp.fl...  21.2 us
  transfers between devices with their start and end apart: 5, of which 1 were waited for; matrix products, arithmetic and copies ran while one was open for 6% of the time, Pallas kernels for 0%

commit v1 on v0

v1 whole, which is shorter than its diff:
```python
import functools

import jax
import jax.numpy as jnp
from jax import lax
from jax.experimental import pallas as pl
from jax.experimental.pallas import tpu as pltpu
from jax.sharding import PartitionSpec as P

MESH = pl.DeviceIdType.MESH
BF16 = jnp.bfloat16
F32 = jnp.float32
KP = 32
CH = 32
LD = 128
CD = 16
SG = 8
NN = (((1,), (0,)), ((), ()))
NT = (((1,), (1,)), ((), ()))


def dot(a, b, dims=NN):
    return lax.dot_general(a, b, dims, preferred_element_type=F32)


def one_hot(row, rows):
    index = lax.broadcasted_iota(jnp.int32, (rows, row.shape[1]), 0)
    return jnp.where(index == row, 1.0, 0.0).astype(BF16)


def lane_iota(rows, lanes):
    return lax.broadcasted_iota(jnp.int32, (rows, lanes), 1)


def fill_member(leaf_ref, member, first):
    member[...] = one_hot(leaf_ref[...] - first, LD)


def fill_basis(basis_ref, basis_pad):
    k = basis_ref.shape[0]
    basis_pad[...] = jnp.zeros_like(basis_pad)
    basis_pad[0:k, :] = basis_ref[...]


def fill_octants(octants):
    for o in range(8):
        lane = lane_iota(1, 128)
        row = (lane >> 4) * 128 + 8 * (lane & 15) + o
        octants[:, o * 128 : (o + 1) * 128] = one_hot(row, 1024)


def spread(values_ref, basis_pad, member, out):
    def block(b, carry):
        values = values_ref[pl.ds(pl.multiple_of(b * 16, 16), 16), :].astype(F32)
        for quad in range(4):
            scaled = jnp.concatenate(
                [
                    (basis_pad[...] * values[c : c + 1, :]).astype(BF16)
                    for c in range(quad * 4, quad * 4 + 4)
                ],
                axis=0,
            )
            row = pl.multiple_of(b * 512 + quad * 128, 128)
            out[pl.ds(row, 128), 0:LD] = dot(scaled, member[...], NT).astype(BF16)
        return carry

    lax.fori_loop(0, CH // 16, block, 0)


def to_parents(fields, octants, ops, stack):
    wide = jnp.concatenate(
        [
            jnp.concatenate(
                [fields[(cb * 8 + c) * KP : (cb * 8 + c + 1) * KP, 0:LD] for c in range(8)], axis=1
            )
            for cb in range(4)
        ],
        axis=0,
    )
    for o in range(8):
        part = dot(wide, octants[:, o * 128 : (o + 1) * 128]).astype(BF16)
        for cb in range(4):
            stack[o * KP : (o + 1) * KP, cb * 128 : (cb + 1) * 128] = part[cb * KP : (cb + 1) * KP]
    return dot(ops, stack[...]).astype(BF16)


def near_kernel(n_chan, cells_axis, *refs):
    (charges_ref, basis_ref, leaf_ref, up_ref, downt_ref, mix_ref, cot_ref) = refs[:7]
    (src_ref, csrc_ref, back_ref, bfar_ref) = refs[7:11]
    (cot_all, basis_pad, member, octants, stack, back_pot, bexp, to_left, to_right, from_right,
     from_left, coarse, coarse_right, coarse_left, sends, recvs) = refs[11:]
    n_cells = cells_axis
    cells = lax.axis_index("cells")
    chan = lax.axis_index("chan")
    left = lax.rem(cells + n_cells - 1, n_cells)
    right = lax.rem(cells + 1, n_cells)
    barrier = pltpu.get_barrier_semaphore()
    for r in range(1, n_chan):
        pl.semaphore_signal(
            barrier, inc=1, device_id=(cells, lax.rem(chan + r, n_chan)), device_id_type=MESH
        )
    for side in (left, right):
        pl.semaphore_signal(barrier, inc=1, device_id=(side, chan), device_id_type=MESH)
    pl.semaphore_wait(barrier, n_chan + 1)

    mine = pl.ds(pl.multiple_of(chan * CH, CH), CH)
    copies = []
    for r in range(1, n_chan):
        copy = pltpu.make_async_remote_copy(
            src_ref=cot_ref,
            dst_ref=cot_all.at[mine, :],
            send_sem=sends.at[r],
            recv_sem=recvs.at[r],
            device_id=(cells, lax.rem(chan + r, n_chan)),
            device_id_type=MESH,
        )
        copy.start()
        copies.append(copy)

    fill_member(leaf_ref, member, cells * LD)
    fill_basis(basis_ref, basis_pad)
    spread(charges_ref, basis_pad, member, src_ref)
    low = lane_iota(512, 128) < 64
    top = src_ref[0:512, 0:LD].astype(F32)
    bottom = pltpu.roll(src_ref[512:1024, 0:LD].astype(F32), 64, 1)
    to_left[...] = jnp.where(low, top, bottom).astype(BF16)
    to_right[...] = jnp.where(low, bottom, top).astype(BF16)
    halo = []
    for i, (source, target, side) in enumerate(
        ((to_left, from_right, left), (to_right, from_left, right))
    ):
        copy = pltpu.make_async_remote_copy(
            src_ref=source,
            dst_ref=target,
            send_sem=sends.at[n_chan + i],
            recv_sem=recvs.at[n_chan + i],
            device_id=(side, chan),
            device_id_type=MESH,
        )
        copy.start()
        halo.append(copy)

    fill_octants(octants)
    coarse[...] = to_parents(src_ref, octants, up_ref[...], stack)
    for i, (target, side) in enumerate(((coarse_right, left), (coarse_left, right))):
        copy = pltpu.make_async_remote_copy(
            src_ref=coarse,
            dst_ref=target,
            send_sem=sends.at[n_chan + 2 + i],
            recv_sem=recvs.at[n_chan + 2 + i],
            device_id=(side, chan),
            device_id_type=MESH,
        )
        copy.start()
        halo.append(copy)

    cot_all[mine, :] = cot_ref[...]
    for copy in copies:
        copy.wait()
    back_pot[...] = dot(mix_ref[mine, :], cot_all[...]).astype(BF16)
    spread(back_pot, basis_pad, member, bexp)
    bfar_ref[...] = to_parents(bexp, octants, downt_ref[...], stack)
    for c in range(CH):
        back_ref[:, c * LD : (c + 1) * LD] = bexp[c * KP : (c + 1) * KP, :]

    for copy in halo:
        copy.wait()
    a, b = from_right[...].astype(F32), from_left[...].astype(F32)
    src_ref[0:512, LD : 2 * LD] = jnp.where(low, a, b).astype(BF16)
    src_ref[512:1024, LD : 2 * LD] = pltpu.roll(jnp.where(low, b, a), 64, 1).astype(BF16)
    first = (lane_iota(KP, 128) & 15) < 8
    for cb in range(4):
        lanes = slice(cb * 128, (cb + 1) * 128)
        rows = slice(cb * KP, (cb + 1) * KP)
        csrc_ref[rows, 0:128] = coarse[:, lanes]
        csrc_ref[rows, 128:256] = jnp.where(
            first, coarse_right[:, lanes].astype(F32), coarse_left[:, lanes].astype(F32)
        ).astype(BF16)


def gather_group(lists, group, source, picked):
    rows = lists[pl.ds(pl.multiple_of(group * SG, SG), SG), :]
    blocks = source.shape[0] // KP
    for pair in range(SG // 2):
        hot = jnp.concatenate(
            [one_hot(rows[s : s + 1, :], 256) for s in (2 * pair, 2 * pair + 1)], axis=1
        )
        for part in range(0, blocks, 4):
            got = dot(source[part * KP : (part + 4) * KP, :], hot).astype(BF16)
            for half in range(2):
                s = 2 * pair + half
                for i in range(4):
                    c = part + i
                    picked[s * KP : (s + 1) * KP, c * 128 : (c + 1) * 128] = got[
                        i * KP : (i + 1) * KP, half * 128 : (half + 1) * 128
                    ]


def field_kernel(*refs):
    (src_ref, csrc_ref, back_ref, bfar_ref, lists_ref, clists_ref, lops_ref, cops_ref, down_ref,
     basis_ref, leaf_ref) = refs[:11]
    (pot_ref, grad_ref) = refs[11:13]
    (lists, clists, picked, cpicked, near, far, slots, expand, basis_pad, member, pot) = refs[13:]
    cells = lax.axis_index("cells")
    n_slots = lists_ref.shape[0]
    groups = n_slots // SG
    k = basis_ref.shape[0]

    raw = lists_ref[...]
    lists[...] = jnp.where(raw < 0, -1, (raw - cells * LD) & 255)
    raw = clists_ref[...]
    at = jnp.where(raw < 0, -1, (raw - cells * CD) & 31)
    c8 = (lane_iota(n_slots, 128) >> 4) * CD
    clists[...] = jnp.where(at < 0, -1, jnp.where(at < CD, c8 + at, 112 + c8 + at))

    far[...] = jnp.zeros_like(far)

    def coarse_group(g, carry):
        gather_group(clists, g, csrc_ref, cpicked)
        ops = cops_ref[:, pl.ds(pl.multiple_of(g * 256, 256), 256)]
        far[...] += dot(ops, cpicked[...])
        row = pl.multiple_of((groups + g) * 256, 256)
        slots[pl.ds(row, 256), 0:KP] = dot(cpicked[...], bfar_ref[...], NT)
        return carry

    lax.fori_loop(0, groups, coarse_group, 0)

    far16 = far[...].astype(BF16)
    far_rows = jnp.concatenate([far16[:, cb * 128 : (cb + 1) * 128] for cb in range(4)], axis=0)
    octant = lane_iota(KP, 128) & 7
    for c in range(8):
        parent = (lane_iota(1, 128) >> 3) + c * CD
        wide = dot(far_rows, one_hot(parent, 128))
        for cb in range(4):
            lanes = slice((cb * 8 + c) * 128, (cb * 8 + c + 1) * 128)
            block = wide[cb * KP : (cb + 1) * KP, :]
            for o in range(8):
                picked[o * KP : (o + 1) * KP, lanes] = jnp.where(octant == o, block, 0.0).astype(BF16)
    for c in range(0, CH * LD, 512):
        near[:, c : c + 512] = dot(down_ref[...], picked[:, c : c + 512])

    def leaf_group(g, carry):
        gather_group(lists, g, src_ref, picked)
        ops = lops_ref[:, pl.ds(pl.multiple_of(g * 256, 256), 256)]
        for c in range(0, CH * LD, 512):
            near[:, c : c + 512] += dot(ops, picked[:, c : c + 512])
        row = pl.multiple_of(g * 256, 256)
        slots[pl.ds(row, 256), 0:KP] = dot(picked[...], back_ref[...], NT)
        return carry

    lax.fori_loop(0, groups, leaf_group, 0)

    for c in range(CH):
        expand[c * KP : (c + 1) * KP, :] = near[:, c * LD : (c + 1) * LD].astype(BF16)
    fill_member(leaf_ref, member, cells * LD)
    fill_basis(basis_ref, basis_pad)

    def collect(b, carry):
        rows = []
        for quad in range(4):
            row = pl.multiple_of(b * 512 + quad * 128, 128)
            per_atom = dot(expand[pl.ds(row, 128), :], member[...])
            for c in range(4):
                rows.append(
                    jnp.sum(
                        per_atom[c * KP : (c + 1) * KP, :] * basis_pad[...], axis=0, keepdims=True
                    )
                )
        pot_ref[pl.ds(pl.multiple_of(b * 16, 16), 16), :] = jnp.concatenate(rows, axis=0).astype(BF16)
        return carry

    lax.fori_loop(0, CH // 16, collect, 0)

    grad_ref[...] = jnp.zeros_like(grad_ref)
    for j in range(k):
        turned = slots[pl.ds(j, 2 * n_slots, stride=KP), :].T
        for i in range(k):
            grad_ref[i * k + j : i * k + j + 1, :] = turned[i : i + 1, :]


def mix_kernel(n_chan, n_x, n_z, k, rc, *refs):
    (pot_ref, grad_ref, charges_ref, mix_ref) = refs[:4]
    (out_ref, gl_ref, gc_ref) = refs[4:7]
    (pot_all, mixt, half_in, half, part_in, part, plane_in, total, send_p, recv_p, send_h, recv_h, send_x,
     recv_x, send_z, recv_z, send_g, recv_g, send_e, recv_e) = refs[7:]
    cells = lax.axis_index("cells")
    chan = lax.axis_index("chan")
    core = lax.rem(cells, 2)
    x = lax.rem(cells // 2, n_x)
    z = cells // (2 * n_x)
    n_plane = n_x * n_chan
    m = x * n_chan + chan
    slots = gl_ref.shape[2]

    other = (cells + 1 - 2 * core, chan)

    def plane_peer(r):
        d = lax.rem(m + r, n_plane)
        return d, ((z * n_x + d // n_chan) * 2 + core, lax.rem(d, n_chan))

    def z_peer(r):
        d = lax.rem(z + r, n_z)
        return d, ((d * n_x + x) * 2 + core, chan)

    barrier = pltpu.get_barrier_semaphore()
    pl.semaphore_signal(barrier, inc=1, device_id=other, device_id_type=MESH)
    for r in range(1, n_plane):
        pl.semaphore_signal(barrier, inc=1, device_id=plane_peer(r)[1], device_id_type=MESH)
    for r in range(1, n_z):
        pl.semaphore_signal(barrier, inc=1, device_id=z_peer(r)[1], device_id_type=MESH)
    pl.semaphore_wait(barrier, n_plane + n_z - 1)

    size = n_plane * rc
    half_copy = pltpu.make_async_remote_copy(
        src_ref=grad_ref.at[pl.ds(pl.multiple_of((1 - core) * size, 8), size), :],
        dst_ref=half_in,
        send_sem=send_h,
        recv_sem=recv_h,
        device_id=other,
        device_id_type=MESH,
    )
    half_copy.start()
    mine = pl.ds(pl.multiple_of(chan * CH, CH), CH)
    pot_copies = []
    for r in range(1, n_chan):
        copy = pltpu.make_async_remote_copy(
            src_ref=pot_ref,
            dst_ref=pot_all.at[mine, :],
            send_sem=send_p.at[r],
            recv_sem=recv_p.at[r],
            device_id=(cells, lax.rem(chan + r, n_chan)),
            device_id_type=MESH,
        )
        copy.start()
        pot_copies.append(copy)
    pot_all[mine, :] = pot_ref[...]
    mixt[...] = mix_ref[...].astype(F32).T.astype(BF16)

    half_copy.wait()
    half[...] = grad_ref[pl.ds(pl.multiple_of(core * size, 8), size), :] + half_in[...]

    def exchange(source_of, target, peers, send, recv):
        copies = []
        for r, (d, device) in peers:
            copy = pltpu.make_async_remote_copy(
                src_ref=source_of(d),
                dst_ref=target(r),
                send_sem=send.at[r],
                recv_sem=recv.at[r],
                device_id=device,
                device_id_type=MESH,
            )
            copy.start()
            copies.append(copy)
        return copies

    def rows(d):
        return pl.ds(pl.multiple_of(d * rc, 8), rc)

    plane = [(r, plane_peer(r)) for r in range(1, n_plane)]
    copies = exchange(lambda d: half.at[rows(d), :], lambda r: part_in.at[r], plane, send_x, recv_x)
    for copy in pot_copies:
        copy.wait()
    out_ref[...] = (
        charges_ref[...].astype(F32) + dot(mixt[mine, :], pot_all[...])
    ).astype(BF16)
    for copy in copies:
        copy.wait()
    summed = half[rows(m), :]
    for r in range(1, n_plane):
        summed = summed + part_in[r]
    part[...] = summed

    copies = exchange(
        lambda d: part, lambda r: plane_in.at[z], [(r, z_peer(r)) for r in range(1, n_z)], send_z, recv_z
    )
    plane_in[z] = part[...]
    for copy in copies:
        copy.wait()
    summed = plane_in[0]
    for r in range(1, n_z):
        summed = summed + plane_in[r]
    first = core * size
    own = pl.ds(pl.multiple_of(first + m * rc, 8), rc)
    total[own, :] = summed

    copies = exchange(lambda d: total.at[own, :], lambda r: total.at[own, :], plane, send_g, recv_g)
    for copy in copies:
        copy.wait()
    side = pl.ds(pl.multiple_of(first, 8), size)
    last = pltpu.make_async_remote_copy(
        src_ref=total.at[side, :],
        dst_ref=total.at[side, :],
        send_sem=send_e,
        recv_sem=recv_e,
        device_id=other,
        device_id_type=MESH,
    )
    last.start()
    last.wait()
    for i in range(k):
        block = total[i * k : (i + 1) * k, :]
        gl_ref[i] = block[:, 0:slots]
        gc_ref[i] = pltpu.roll(block, 128 - slots, 1)[:, 0:slots]


def ops_rows(ops, pad_out):
    k, _, s = ops.shape
    turned = jnp.pad(jnp.transpose(ops, (0, 2, 1)), ((0, KP - k), (0, 0), (0, KP - k)))
    return turned.reshape(KP, s * KP)


def octant_rows(ops):
    o, k, _ = ops.shape
    return jnp.pad(jnp.transpose(ops, (1, 0, 2)), ((0, KP - k), (0, 0), (0, KP - k))).reshape(KP, o * KP)


VMEM = pl.BlockSpec(memory_space=pltpu.VMEM)


def call(kernel, outs, scratch, args, collective=None):
    extra = {}
    if collective is not None:
        extra = dict(collective_id=collective, has_side_effects=True)
    return pl.pallas_call(
        kernel,
        out_shape=outs,
        in_specs=[VMEM] * len(args),
        out_specs=[VMEM] * len(outs),
        scratch_shapes=scratch,
        compiler_params=pltpu.CompilerParams(vmem_limit_bytes=60 << 20, **extra),
    )(*args)


def local(n_cells, n_chan, n_x, n_z, charges, basis, atom_leaf, leaf_lists, coarse_lists, up_ops, down_ops, leaf_ops,
          coarse_ops, mix, cotangent):
    k, atoms = basis.shape
    slots = leaf_lists.shape[0]
    shape = jax.ShapeDtypeStruct
    dma = pltpu.SemaphoreType.DMA
    leaf_row = atom_leaf.reshape(1, atoms)
    n_plane = n_x * n_chan
    rc = -(-k * k // (16 * n_plane)) * 8

    src, csrc, back, bfar = call(
        functools.partial(near_kernel, n_chan, n_cells),
        [
            shape((CH * KP, 2 * LD), BF16),
            shape((4 * KP, 256), BF16),
            shape((KP, CH * LD), BF16),
            shape((KP, CH * CD), BF16),
        ],
        [
            pltpu.VMEM((n_chan * CH, atoms), BF16),
            pltpu.VMEM((KP, atoms), F32),
            pltpu.VMEM((LD, atoms), BF16),
            pltpu.VMEM((1024, 1024), BF16),
            pltpu.VMEM((8 * KP, CH * CD), BF16),
            pltpu.VMEM((CH, atoms), BF16),
            pltpu.VMEM((CH * KP, LD), BF16),
            pltpu.VMEM((512, LD), BF16),
            pltpu.VMEM((512, LD), BF16),
            pltpu.VMEM((512, LD), BF16),
            pltpu.VMEM((512, LD), BF16),
            pltpu.VMEM((KP, CH * CD), BF16),
            pltpu.VMEM((KP, CH * CD), BF16),
            pltpu.VMEM((KP, CH * CD), BF16),
            dma((n_chan + 4,)),
            dma((n_chan + 4,)),
        ],
        (charges, basis, leaf_row, octant_rows(up_ops), octant_rows(jnp.transpose(down_ops, (0, 2, 1))), mix,
         cotangent),
        collective=0,
    )

    pot, grads = call(
        field_kernel,
        [shape((CH, atoms), BF16), shape((2 * n_plane * rc, 128), F32)],
        [
            pltpu.VMEM((slots, LD), jnp.int32),
            pltpu.VMEM((slots, 128), jnp.int32),
            pltpu.VMEM((SG * KP, CH * LD), BF16),
            pltpu.VMEM((SG * KP, CH * CD), BF16),
            pltpu.VMEM((KP, CH * LD), F32),
            pltpu.VMEM((KP, CH * CD), F32),
            pltpu.VMEM((2 * slots * KP, 128), F32),
            pltpu.VMEM((CH * KP, LD), BF16),
            pltpu.VMEM((KP, atoms), F32),
            pltpu.VMEM((LD, atoms), BF16),
            pltpu.VMEM((CH, atoms), F32),
        ],
        (src, csrc, back, bfar, leaf_lists, jnp.tile(coarse_lists, (1, 8)), ops_rows(leaf_ops, KP),
         ops_rows(coarse_ops, KP), octant_rows(down_ops), basis, leaf_row),
    )

    refined, gl, gc = call(
        functools.partial(mix_kernel, n_chan, n_x, n_z, k, rc),
        [shape((CH, atoms), BF16), shape((k, k, slots), F32), shape((k, k, slots), F32)],
        [
            pltpu.VMEM((n_chan * CH, atoms), BF16),
            pltpu.VMEM(mix.shape, BF16),
            pltpu.VMEM((n_plane * rc, 128), F32),
            pltpu.VMEM((n_plane * rc, 128), F32),
            pltpu.VMEM((n_plane, rc, 128), F32),
            pltpu.VMEM((rc, 128), F32),
            pltpu.VMEM((n_z, rc, 128), F32),
            pltpu.VMEM((2 * n_plane * rc, 128), F32),
            dma((n_chan,)),
            dma((n_chan,)),
            dma,
            dma,
            dma((n_plane,)),
            dma((n_plane,)),
            dma((n_z,)),
            dma((n_z,)),
            dma((n_plane,)),
            dma((n_plane,)),
            dma,
            dma,
        ],
        (pot, grads, charges, mix),
        collective=1,
    )
    return refined, gl, gc


def solution(mesh):
    n_cells, n_chan = mesh.shape["cells"], mesh.shape["chan"]
    n_x = 4 if n_cells % 8 == 0 and n_cells > 8 else 2
    n_z = n_cells // (2 * n_x)
    placed = (
        P("chan", "cells"),
        P(None, "cells"),
        P("cells"),
        P(None, "cells"),
        P(None, "cells"),
        P(),
        P(),
        P(),
        P(),
        P(),
        P("chan", "cells"),
    )
    return jax.shard_map(
        functools.partial(local, n_cells, n_chan, n_x, n_z),
        mesh=mesh,
        in_specs=placed,
        out_specs=(P("chan", "cells"), P(), P()),
        check_vma=False,
    )
```

time: 726 us -> 77.8 us (0.11)
  local copies, waits for them, and re-layouts: 352 us -> 11.3 us
  waiting for transfers between devices: 269 us -> 0 us
  Pallas kernels: 0 us -> 65.4 us
  matrix products: 49.3 us -> 0 us
  blocking collectives: 18.7 us -> 0 us
  between operations: 14.3 us -> 0.72 us
  starting transfers between devices: 12.6 us -> 0 us
    gather x32 -> x0, local copies, waits for them, and re-layouts: 325 us -> none  [pick(): picked = jnp.take(source, position, axis=2)]
    psum x1 -> x0, waiting for transfers between devices: 269 us -> none  [local(): lax.psum((grad_leaf, grad_coarse), ('cells', 'chan'))]
    pallas_call x0 -> x3, Pallas kernels: none -> 65.4 us  [call(): pl.pallas_call(kernel, out_shape=outs, in_specs=[VMEM] * len(args), out_s...]
    dot_general x24 -> x0, matrix products: 49.3 us -> none  [the longest x8 22.9 us: translate_advance(): jnp.einsum('okj,jcot->kct', group_ops, picked, preferred_element_type=jnp...]
    all_gather x2 -> x0, blocking collectives: 18.7 us -> none  [the longest x1 9.37 us: local(): lax.all_gather(cotangent, 'chan', axis=0, tiled=True)]
    ppermute x4 -> x0, starting transfers between devices: 12.6 us -> none  [the longest x2 8.17 us: extended(): lax.ppermute(lax.slice_in_dim(block, 0, width, axis=dim), axis, backward)]
  transfers between devices with their start and end apart: 5 -> 0, of which waited for: 1 -> 0; matrix products, arithmetic and copies ran while one was open for 6% -> 0% of each run, Pallas kernels for 0% -> 0%
where the time goes in v1:
time: 77.8 us; the launch traced here: 77.4 us
  Pallas kernels  65.4 us (84%)
  local copies, waits for them, and re-layouts  11.3 us (15%)
    pallas_call x3, Pallas kernels, call(): pl.pallas_call(kernel, out_shape=outs, in_specs=[VMEM] * len(args), out_s...  65.4 us
    unnamed x18, local copies, waits for them, and re-layouts  5.77 us
    reshape x2, local copies, waits for them, and re-layouts, ops_rows(): return turned.reshape(KP, s * KP)  2.39 us
    reshape x3, local copies, waits for them, and re-layouts, octant_rows(): jnp.pad(jnp.transpose(ops, (1, 0, 2)), ((0, KP - k), (0, 0), (0, KP - k)))  2.14 us

profile of v1, /device:TPU:1, one launch (start us, length us, event | category | flops | bytes accessed | tf_op | source)
XLA Modules:
  0.0 77.4 jit_solution(14878991349100480770)
XLA Ops:
  0.6 1.0 %copy.22 = bf16[25,8,25]{2,1,0:T(8,128)(2,1)S(1)} copy(bf16[25,8,25]{0,1,2:T(8,128)(2,1)} %bitcast.8) | data formatting | bytes 20000
  1.6 0.0 copy-start.5
  1.6 0.7 reshape.30.refs_4_
  2.3 0.0 copy-done.5
  2.3 0.0 copy-start.4
  2.4 0.7 copy.21.refs_5_
  3.1 0.1 copy-done.4
  3.2 0.0 copy-start.1
  3.2 0.0 copy-start.2
  3.2 0.7 reshape.29.refs_3_
  3.9 0.1 copy-done.1
  4.0 0.7 reshape.33.refs_8_
  4.7 0.0 copy-done.2
  4.7 0.3 copy.23
  5.0 0.1 pad.19.clone
  5.1 0.0 copy-start.3
  5.1 1.2 %reshape.31.refs_6_ = bf16[32,2048]{1,0:T(8,128)(2,1)} reshape(bf16[32,64,32]{2,1,0:T(8,128)(2,1)S(1)} %pad.19.clone) | data formatting | bytes 262144 | tf_op jit(solution)/shard_map/reshape | solution.py:410
  6.3 0.0 copy-done.3
  6.3 0.3 copy.24
  6.6 0.1 pad.20.clone
  6.7 1.2 %reshape.32.refs_7_ = bf16[32,2048]{1,0:T(8,128)(2,1)} reshape(bf16[32,64,32]{2,1,0:T(8,128)(2,1)S(1)} %pad.20.clone) | data formatting | bytes 262144 | tf_op jit(solution)/shard_map/reshape | solution.py:410
  7.9 14.2 %shard_map.130 = (bf16[1024,256]{1,0:T(8,128)(2,1)}, bf16[128,256]{1,0:T(8,128)(2,1)}, bf16[32,4096]{1,0:T(8,128)(2,1)}, bf16[32,512]{1,0:T(8,128)(2,1)}) custom-call(bf16[32,1024]{1,0:T(8,128)(2,1)} %refs_2_.1, f32[25,1024]{1,0:T(8,128)} %refs_9_.1, s32[1,1024]{1,0:T(1,128)} %bitcast.13, bf16[32,256]{1,0:T(8,128)(2,1)} %reshape.29.refs_3_, ...), custom_call_target="tpu_custom_call" | custom-call | tf_op jit(solution)/shard_map/pallas_call | solution.py:425
  22.2 21.6 %shard_map.131 = (bf16[32,1024]{1,0:T(8,128)(2,1)}, f32[768,128]{1,0:T(8,128)}) custom-call(bf16[1024,256]{1,0:T(8,128)(2,1)} %get-tuple-element.9.refs_0_, bf16[128,256]{1,0:T(8,128)(2,1)} %get-tuple-element.10.refs_1_, bf16[32,4096]{1,0:T(8,128)(2,1)} %get-tuple-element.11.refs_2_, bf16[32,512]{1,0:T(8,128)(2,1)} %get-tuple-element.12.refs_3_, ...), custom_call_target="tpu_custom_call" | custom-call | tf_op jit(solution)/shard_map/pallas_call | solution.py:425
  43.7 29.6 %shard_map.132 = (bf16[32,1024]{1,0:T(8,128)(2,1)}, f32[25,25,64]{2,1,0:T(8,128)}, f32[25,25,64]{2,1,0:T(8,128)}) custom-call(bf16[32,1024]{1,0:T(8,128)(2,1)} %get-tuple-element.13.refs_0_, f32[768,128]{1,0:T(8,128)} %get-tuple-element.14.refs_1_, bf16[32,1024]{1,0:T(8,128)(2,1)} %refs_2_.1, bf16[128,128]{1,0:T(8,128)(2,1)} %refs_3_.1), custom_call_target="tpu_custom_call" | custom-call | tf_op jit(solution)/shard_map/pallas_call | solution.py:425
  73.4 1.5 %copy.28 = bf16[32,1024]{1,0:T(8,128)(2,1)} copy(bf16[32,1024]{1,0:T(8,128)(2,1)} %get-tuple-element.18) | data formatting | bytes 131072
  74.8 0.0 copy-start
  74.8 1.8 %copy.29 = f32[25,25,64]{2,1,0:T(8,128)} copy(f32[25,25,64]{2,1,0:T(8,128)} %get-tuple-element.19) | data formatting | bytes 320000
  76.7 0.0 copy-done
  76.7 0.8 copy.30
  (4 shorter events, 0.1 us)
Async XLA Ops:
  1.6 0.7 copy-start.5
  2.3 0.8 %copy-start.4 = (bf16[8,25,25]{2,0,1:T(8,128)(2,1)S(1)}, bf16[8,25,25]{2,0,1:T(8,128)(2,1)}, u32[]{:S(2)}) copy-start(bf16[8,25,25]{2,0,1:T(8,128)(2,1)} %param.16) | copy-start | bytes 30004
  3.2 0.8 %copy-start.1 = (bf16[8,25,25]{2,0,1:T(8,128)(2,1)S(1)}, bf16[8,25,25]{2,0,1:T(8,128)(2,1)}, u32[]{:S(2)}) copy-start(bf16[8,25,25]{2,0,1:T(8,128)(2,1)} %param.17) | copy-start | bytes 30004
  3.2 1.5 %copy-start.2 = (bf16[25,25,64]{2,1,0:T(8,128)(2,1)S(1)}, bf16[25,25,64]{2,1,0:T(8,128)(2,1)}, u32[]{:S(2)}) copy-start(bf16[25,25,64]{2,1,0:T(8,128)(2,1)} %param.18) | copy-start | bytes 240004
  5.1 1.2 %copy-start.3 = (bf16[25,25,64]{2,1,0:T(8,128)(2,1)S(1)}, bf16[25,25,64]{2,1,0:T(8,128)(2,1)}, u32[]{:S(2)}) copy-start(bf16[25,25,64]{2,1,0:T(8,128)(2,1)} %param.19) | copy-start | bytes 240004
  74.8 1.8 %copy-start = (f32[25,25,64]{2,1,0:T(8,128)S(1)}, f32[25,25,64]{2,1,0:T(8,128)}, u32[]{:S(2)}) copy-start(f32[25,25,64]{2,1,0:T(8,128)} %get-tuple-element.20) | copy-start | bytes 480004

commit v2 on v0

v2 whole, which is shorter than its diff:
```python
import functools

import jax
import jax.numpy as jnp
from jax import lax
from jax.experimental import pallas as pl
from jax.experimental.pallas import tpu as pltpu
from jax.sharding import PartitionSpec as P

MESH = pl.DeviceIdType.MESH
BF16 = jnp.bfloat16
F32 = jnp.float32
KP = 32
CH = 32
LD = 128
CD = 16
SG = 8
NN = (((1,), (0,)), ((), ()))
NT = (((1,), (1,)), ((), ()))
TN = (((0,), (0,)), ((), ()))


def dot(a, b, dims=NN):
    return lax.dot_general(a, b, dims, preferred_element_type=F32)


def one_hot(row, rows):
    index = lax.broadcasted_iota(jnp.int32, (rows, row.shape[1]), 0)
    return jnp.where(index == row, 1.0, 0.0).astype(BF16)


def lane_iota(rows, lanes):
    return lax.broadcasted_iota(jnp.int32, (rows, lanes), 1)


def fill_member(leaf_ref, member, first):
    member[...] = one_hot(leaf_ref[...] - first, LD)


def fill_basis(basis_ref, basis_pad):
    k = basis_ref.shape[0]
    basis_pad[...] = jnp.zeros_like(basis_pad)
    basis_pad[0:k, :] = basis_ref[...]


def fill_octants(octants):
    for o in range(8):
        lane = lane_iota(1, 128)
        row = (lane >> 4) * 128 + 8 * (lane & 15) + o
        octants[:, o * 128 : (o + 1) * 128] = one_hot(row, 1024)


def spread(values_ref, basis_pad, member, out):
    def block(b, carry):
        values = values_ref[pl.ds(pl.multiple_of(b * 16, 16), 16), :].astype(F32)
        for quad in range(4):
            scaled = jnp.concatenate(
                [
                    (basis_pad[...] * values[c : c + 1, :]).astype(BF16)
                    for c in range(quad * 4, quad * 4 + 4)
                ],
                axis=0,
            )
            row = pl.multiple_of(b * 512 + quad * 128, 128)
            out[pl.ds(row, 128), 0:LD] = dot(scaled, member[...], NT).astype(BF16)
        return carry

    lax.fori_loop(0, CH // 16, block, 0)


def to_parents(fields, octants, ops, dims, stack):
    wide = jnp.concatenate(
        [
            jnp.concatenate(
                [fields[(cb * 8 + c) * KP : (cb * 8 + c + 1) * KP, 0:LD] for c in range(8)], axis=1
            )
            for cb in range(4)
        ],
        axis=0,
    )
    for o in range(8):
        part = dot(wide, octants[:, o * 128 : (o + 1) * 128]).astype(BF16)
        for cb in range(4):
            stack[o * KP : (o + 1) * KP, cb * 128 : (cb + 1) * 128] = part[cb * KP : (cb + 1) * KP]
    return dot(ops, stack[...], dims).astype(BF16)


def gather_group(lists, group, source, picked, base):
    rows = lists[pl.ds(pl.multiple_of(group * SG, SG), SG), :]
    blocks = source.shape[0] // KP
    for pair in range(SG // 2):
        hot = jnp.concatenate(
            [one_hot(rows[s : s + 1, :], 256) for s in (2 * pair, 2 * pair + 1)], axis=1
        )
        for part in range(0, blocks, 4):
            got = dot(source[part * KP : (part + 4) * KP, :], hot).astype(BF16)
            for half in range(2):
                s = 2 * pair + half
                for i in range(4):
                    c = part + i
                    picked[pl.ds(base + s * KP, KP), c * 128 : (c + 1) * 128] = got[
                        i * KP : (i + 1) * KP, half * 128 : (half + 1) * 128
                    ]


def group_rows(g):
    return pl.ds(pl.multiple_of(g * SG * KP, SG * KP), SG * KP)


def turn_ops(leaf_ops_ref, coarse_ops_ref, rows, turned, ops):
    k, _, s = leaf_ops_ref.shape
    rows[...] = jnp.zeros_like(rows)
    turned[...] = jnp.zeros_like(turned)
    for i in range(k):
        both = jnp.concatenate([leaf_ops_ref[i].astype(F32), coarse_ops_ref[i].astype(F32)], axis=1)
        rows[i * KP : i * KP + k, :] = both
    for j in range(k):
        turned[pl.ds(j, 2 * s, stride=KP), 0:KP] = rows[pl.ds(j, KP, stride=KP), :].T
    ops[...] = turned[:, 0:KP].astype(BF16)


def main_kernel(n_cells, n_chan, n_x, n_z, rc, names, *refs):
    r = dict(zip(names, refs))
    cells = lax.axis_index("cells")
    chan = lax.axis_index("chan")
    core = lax.rem(cells, 2)
    x = lax.rem(cells // 2, n_x)
    z = cells // (2 * n_x)
    n_plane = n_x * n_chan
    m = x * n_chan + chan
    k = r["basis"].shape[0]
    n_slots = r["leaf_lists"].shape[0]
    groups = n_slots // SG
    left = (lax.rem(cells + n_cells - 1, n_cells), chan)
    right = (lax.rem(cells + 1, n_cells), chan)
    other = (cells + 1 - 2 * core, chan)
    chan_peers = [(cells, lax.rem(chan + i, n_chan)) for i in range(1, n_chan)]
    plane_peers, z_peers = [], []
    for i in range(1, n_plane):
        d = lax.rem(m + i, n_plane)
        plane_peers.append((d, ((z * n_x + d // n_chan) * 2 + core, lax.rem(d, n_chan))))
    for i in range(1, n_z):
        d = lax.rem(z + i, n_z)
        z_peers.append((d, ((d * n_x + x) * 2 + core, chan)))

    barrier = pltpu.get_barrier_semaphore()
    greeted = chan_peers + [left, right, other] + [d for _, d in plane_peers] + [d for _, d in z_peers]
    for device in greeted:
        pl.semaphore_signal(barrier, inc=1, device_id=device, device_id_type=MESH)

    sems = {"next": 0}

    def send(source, target, device):
        i = sems["next"]
        sems["next"] = i + 1
        copy = pltpu.make_async_remote_copy(
            src_ref=source,
            dst_ref=target,
            send_sem=r["sends"].at[i],
            recv_sem=r["recvs"].at[i],
            device_id=device,
            device_id_type=MESH,
        )
        copy.start()
        return copy

    member, basis_pad, src, bexp = r["member"], r["basis_pad"], r["src"], r["bexp"]
    fill_member(r["leaf"], member, cells * LD)
    fill_basis(r["basis"], basis_pad)
    pl.semaphore_wait(barrier, len(greeted))

    mine = pl.ds(pl.multiple_of(chan * CH, CH), CH)
    cot_copies = [send(r["cot"], r["cot_all"].at[mine, :], d) for d in chan_peers]

    spread(r["charges"], basis_pad, member, src)
    low = lane_iota(512, 128) < 64
    top = src[0:512, 0:LD].astype(F32)
    bottom = pltpu.roll(src[512:1024, 0:LD].astype(F32), 64, 1)
    r["to_left"][...] = jnp.where(low, top, bottom).astype(BF16)
    r["to_right"][...] = jnp.where(low, bottom, top).astype(BF16)
    halo = [send(r["to_left"], r["from_right"], left), send(r["to_right"], r["from_left"], right)]

    for ops_ref, pad in ((r["up"], r["up_pad"]), (r["down"], r["down_pad"])):
        pad[...] = jnp.zeros_like(pad)
        for o in range(8):
            pad[o * KP : o * KP + k, 0:k] = ops_ref[o].astype(F32)
    fill_octants(r["octants"])

    up_wide = jnp.concatenate([r["up_pad"][o * KP : (o + 1) * KP, :] for o in range(8)], axis=1).astype(BF16)
    down_wide = jnp.concatenate([r["down_pad"][o * KP : (o + 1) * KP, :] for o in range(8)], axis=1).astype(BF16)
    down_tall = r["down_pad"][...].astype(BF16)

    coarse = r["coarse"]
    coarse[...] = to_parents(src, r["octants"], up_wide, NN, r["stack"])
    coarse_halo = [send(coarse, r["coarse_right"], left), send(coarse, r["coarse_left"], right)]

    turn_ops(r["leaf_ops"], r["coarse_ops"], r["total"], r["slots"], r["ops"])

    raw = r["leaf_lists"][...]
    r["lists"][...] = jnp.where(raw < 0, -1, (raw - cells * LD) & 255)
    raw = r["coarse_lists"][...]
    raw = jnp.concatenate([raw] * 8, axis=1)
    at = jnp.where(raw < 0, -1, (raw - cells * CD) & 31)
    c8 = (lane_iota(n_slots, 128) >> 4) * CD
    r["clists"][...] = jnp.where(at < 0, -1, jnp.where(at < CD, c8 + at, 112 + c8 + at))

    r["cot_all"][mine, :] = r["cot"][...]
    for copy in cot_copies:
        copy.wait()
    r["back_pot"][...] = dot(r["mix"][mine, :], r["cot_all"][...]).astype(BF16)
    spread(r["back_pot"], basis_pad, member, bexp)
    r["bfar"][...] = to_parents(bexp, r["octants"], down_tall, TN, r["stack"])
    for c in range(CH):
        r["back"][:, c * LD : (c + 1) * LD] = bexp[c * KP : (c + 1) * KP, :]

    for copy in coarse_halo:
        copy.wait()
    first = (lane_iota(KP, 128) & 15) < 8
    csrc = r["csrc"]
    for cb in range(4):
        lanes = slice(cb * 128, (cb + 1) * 128)
        rows = slice(cb * KP, (cb + 1) * KP)
        csrc[rows, 0:128] = coarse[:, lanes]
        csrc[rows, 128:256] = jnp.where(
            first, r["coarse_right"][:, lanes].astype(F32), r["coarse_left"][:, lanes].astype(F32)
        ).astype(BF16)

    picked, cpicked, slots = r["picked"], r["cpicked"], r["slots"]

    def coarse_group(g, carry):
        base = pl.multiple_of(g * SG * KP, SG * KP)
        gather_group(r["clists"], g, csrc, cpicked, base)
        slots[group_rows(groups + g), 0:KP] = dot(cpicked[group_rows(g), :], r["bfar"][...], NT)
        return carry

    lax.fori_loop(0, groups, coarse_group, 0)

    for copy in halo:
        copy.wait()
    a, b = r["from_right"][...].astype(F32), r["from_left"][...].astype(F32)
    src[0:512, LD : 2 * LD] = jnp.where(low, a, b).astype(BF16)
    src[512:1024, LD : 2 * LD] = pltpu.roll(jnp.where(low, b, a), 64, 1).astype(BF16)

    def leaf_group(g, carry):
        base = pl.multiple_of(g * SG * KP, SG * KP)
        gather_group(r["lists"], g, src, picked, base)
        slots[group_rows(g), 0:KP] = dot(picked[group_rows(g), :], r["back"][...], NT)
        return carry

    lax.fori_loop(0, groups, leaf_group, 0)

    grad = r["grad"]
    size = n_plane * rc
    grad[2 * size - 8 * ((2 * size - k * k) // 8) - 8 :, :] = jnp.zeros(
        (8 * ((2 * size - k * k) // 8) + 8, 128), F32
    )
    for j in range(k):
        turned = slots[pl.ds(j, 2 * n_slots, stride=KP), :].T
        grad[pl.ds(j, k, stride=k), :] = turned[0:k, :]
    half_copy = send(
        grad.at[pl.ds(pl.multiple_of((1 - core) * size, 8), size), :], r["half_in"], other
    )

    near, far = r["near"], r["far"]
    far[...] = jnp.zeros_like(far)

    def far_group(g, carry):
        far[...] += dot(r["ops"][group_rows(groups + g), :], cpicked[group_rows(g), :], TN)
        return carry

    lax.fori_loop(0, groups, far_group, 0)
    half_copy.wait()
    half = r["half"]
    half[...] = grad[pl.ds(pl.multiple_of(core * size, 8), size), :] + r["half_in"][...]

    def chunk(d):
        return pl.ds(pl.multiple_of(d * rc, 8), rc)

    plane_copies = [
        send(half.at[chunk(d), :], r["part_in"].at[i], device)
        for i, (d, device) in enumerate(plane_peers)
    ]

    far16 = far[...].astype(BF16)
    far_rows = jnp.concatenate([far16[:, cb * 128 : (cb + 1) * 128] for cb in range(4)], axis=0)
    octant = lane_iota(KP, 128) & 7
    child = r["child"]
    for c in range(8):
        parent = (lane_iota(1, 128) >> 3) + c * CD
        wide = dot(far_rows, one_hot(parent, 128))
        for cb in range(4):
            lanes = slice((cb * 8 + c) * 128, (cb * 8 + c + 1) * 128)
            block = wide[cb * KP : (cb + 1) * KP, :]
            for o in range(8):
                child[o * KP : (o + 1) * KP, lanes] = jnp.where(octant == o, block, 0.0).astype(BF16)
    for c in range(0, CH * LD, 512):
        near[:, c : c + 512] = dot(down_wide, child[:, c : c + 512])

    def near_group(g, carry):
        ops = r["ops"][group_rows(g), :]
        for c in range(0, CH * LD, 512):
            near[:, c : c + 512] += dot(ops, picked[group_rows(g), c : c + 512], TN)
        return carry

    lax.fori_loop(0, groups // 2, near_group, 0)

    for copy in plane_copies:
        copy.wait()
    summed = half[chunk(m), :]
    for i in range(n_plane - 1):
        summed = summed + r["part_in"][i]
    r["part"][...] = summed
    z_copies = [send(r["part"], r["z_in"].at[z], device) for _, device in z_peers]
    r["z_in"][z] = summed

    lax.fori_loop(groups // 2, groups, near_group, 0)

    for copy in z_copies:
        copy.wait()
    summed = r["z_in"][0]
    for i in range(1, n_z):
        summed = summed + r["z_in"][i]
    total = r["total_out"]
    own = pl.ds(pl.multiple_of(core * size + m * rc, 8), rc)
    total[own, :] = summed
    gather_copies = [send(total.at[own, :], total.at[own, :], device) for _, device in plane_peers]

    expand = bexp
    for c in range(CH):
        expand[c * KP : (c + 1) * KP, :] = near[:, c * LD : (c + 1) * LD].astype(BF16)

    def collect(b, carry):
        rows = []
        for quad in range(4):
            row = pl.multiple_of(b * 512 + quad * 128, 128)
            per_atom = dot(expand[pl.ds(row, 128), :], member[...])
            for c in range(4):
                rows.append(
                    jnp.sum(
                        per_atom[c * KP : (c + 1) * KP, :] * basis_pad[...], axis=0, keepdims=True
                    )
                )
        pot[pl.ds(pl.multiple_of(b * 16, 16), 16), :] = jnp.concatenate(rows, axis=0).astype(BF16)
        return carry

    pot = r["pot"]
    lax.fori_loop(0, CH // 16, collect, 0)
    pot_all = r["pot_all"]
    pot_copies = [send(pot, pot_all.at[mine, :], d) for d in chan_peers]
    pot_all[mine, :] = pot[...]

    for copy in gather_copies:
        copy.wait()
    side = pl.ds(pl.multiple_of(core * size, 8), size)
    last = send(total.at[side, :], total.at[side, :], other)
    for copy in pot_copies:
        copy.wait()
    last.wait()


def final_kernel(pot_ref, total_ref, charges_ref, mix_ref, out_ref, gl_ref, gc_ref, mixt):
    chan = lax.axis_index("chan")
    k, _, slots = gl_ref.shape
    mixt[...] = mix_ref[...].astype(F32).T.astype(BF16)
    mine = pl.ds(pl.multiple_of(chan * CH, CH), CH)
    out_ref[...] = (charges_ref[...].astype(F32) + dot(mixt[mine, :], pot_ref[...])).astype(BF16)
    for i in range(k):
        block = total_ref[i * k : (i + 1) * k, :]
        gl_ref[i] = block[:, 0:slots]
        gc_ref[i] = pltpu.roll(block, 128 - slots, 1)[:, 0:slots]


VMEM = pl.BlockSpec(memory_space=pltpu.VMEM)


def call(kernel, outs, scratch, args, collective=None):
    extra = {}
    if collective is not None:
        extra = dict(collective_id=collective, has_side_effects=True)
    return pl.pallas_call(
        kernel,
        out_shape=outs,
        in_specs=[VMEM] * len(args),
        out_specs=[VMEM] * len(outs),
        scratch_shapes=scratch,
        compiler_params=pltpu.CompilerParams(vmem_limit_bytes=60 << 20, **extra),
    )(*args)


def local(n_cells, n_chan, n_x, n_z, charges, basis, atom_leaf, leaf_lists, coarse_lists, up_ops, down_ops, leaf_ops,
          coarse_ops, mix, cotangent):
    k, atoms = basis.shape
    slots = leaf_lists.shape[0]
    shape = jax.ShapeDtypeStruct
    n_plane = n_x * n_chan
    rc = -(-k * k // (16 * n_plane)) * 8
    args = dict(
        charges=charges, basis=basis, leaf=atom_leaf.reshape(1, atoms), leaf_lists=leaf_lists,
        coarse_lists=coarse_lists, up=up_ops, down=down_ops, leaf_ops=leaf_ops, coarse_ops=coarse_ops,
        mix=mix, cot=cotangent,
    )
    outs = dict(
        pot_all=shape((n_chan * CH, atoms), BF16),
        total_out=shape((2 * n_plane * rc, 128), F32),
    )
    copies = 2 * (n_chan - 1) + 4 + 2 + 2 * (n_plane - 1) + n_z - 1
    scratch = dict(
        cot_all=((n_chan * CH, atoms), BF16),
        basis_pad=((KP, atoms), F32),
        member=((LD, atoms), BF16),
        octants=((1024, 1024), BF16),
        stack=((8 * KP, CH * CD), BF16),
        back_pot=((CH, atoms), BF16),
        src=((CH * KP, 2 * LD), BF16),
        csrc=((4 * KP, 256), BF16),
        bexp=((CH * KP, LD), BF16),
        back=((KP, CH * LD), BF16),
        bfar=((KP, CH * CD), BF16),
        to_left=((512, LD), BF16),
        to_right=((512, LD), BF16),
        from_right=((512, LD), BF16),
        from_left=((512, LD), BF16),
        coarse=((KP, CH * CD), BF16),
        coarse_right=((KP, CH * CD), BF16),
        coarse_left=((KP, CH * CD), BF16),
        up_pad=((8 * KP, KP), F32),
        down_pad=((8 * KP, KP), F32),
        lists=((slots, LD), jnp.int32),
        clists=((slots, 128), jnp.int32),
        picked=((slots * KP, CH * LD), BF16),
        cpicked=((slots * KP, CH * CD), BF16),
        child=((8 * KP, CH * LD), BF16),
        near=((KP, CH * LD), F32),
        far=((KP, CH * CD), F32),
        total=((KP * KP, 128), F32),
        slots=((2 * slots * KP, 128), F32),
        ops=((2 * slots * KP, KP), BF16),
        grad=((2 * n_plane * rc, 128), F32),
        half_in=((n_plane * rc, 128), F32),
        half=((n_plane * rc, 128), F32),
        part_in=((n_plane - 1, rc, 128), F32),
        part=((rc, 128), F32),
        z_in=((n_z, rc, 128), F32),
        pot=((CH, atoms), BF16),
    )
    names = tuple(args) + tuple(outs) + tuple(scratch) + ("sends", "recvs")
    pot_all, total = call(
        functools.partial(main_kernel, n_cells, n_chan, n_x, n_z, rc, names),
        list(outs.values()),
        [pltpu.VMEM(*v) for v in scratch.values()] + [pltpu.SemaphoreType.DMA((copies,))] * 2,
        tuple(args.values()),
        collective=0,
    )
    return call(
        final_kernel,
        [shape((CH, atoms), BF16), shape((k, k, slots), F32), shape((k, k, slots), F32)],
        [pltpu.VMEM(mix.shape, BF16)],
        (pot_all, total, charges, mix),
    )


def solution(mesh):
    n_cells, n_chan = mesh.shape["cells"], mesh.shape["chan"]
    n_x = 4 if n_cells % 8 == 0 and n_cells > 8 else 2
    n_z = n_cells // (2 * n_x)
    placed = (
        P("chan", "cells"),
        P(None, "cells"),
        P("cells"),
        P(None, "cells"),
        P(None, "cells"),
        P(),
        P(),
        P(),
        P(),
        P(),
        P("chan", "cells"),
    )
    return jax.shard_map(
        functools.partial(local, n_cells, n_chan, n_x, n_z),
        mesh=mesh,
        in_specs=placed,
        out_specs=(P("chan", "cells"), P(), P()),
        check_vma=False,
    )
```

time: 726 us -> 62.7 us (0.09)
  local copies, waits for them, and re-layouts: 352 us -> 3.49 us
  waiting for transfers between devices: 269 us -> 0 us
  Pallas kernels: 0 us -> 58.3 us
  matrix products: 49.3 us -> 0 us
  blocking collectives: 18.7 us -> 0 us
  between operations: 14.3 us -> 0.64 us
  starting transfers between devices: 12.6 us -> 0 us
    gather x32 -> x0, local copies, waits for them, and re-layouts: 325 us -> none  [pick(): picked = jnp.take(source, position, axis=2)]
    psum x1 -> x0, waiting for transfers between devices: 269 us -> none  [local(): lax.psum((grad_leaf, grad_coarse), ('cells', 'chan'))]
    pallas_call x0 -> x2, Pallas kernels: none -> 58.3 us  [call(): pl.pallas_call(kernel, out_shape=outs, in_specs=[VMEM] * len(args), out_s...]
    dot_general x24 -> x0, matrix products: 49.3 us -> none  [the longest x8 22.9 us: translate_advance(): jnp.einsum('okj,jcot->kct', group_ops, picked, preferred_element_type=jnp...]
    all_gather x2 -> x0, blocking collectives: 18.7 us -> none  [the longest x1 9.37 us: local(): lax.all_gather(cotangent, 'chan', axis=0, tiled=True)]
    ppermute x4 -> x0, starting transfers between devices: 12.6 us -> none  [the longest x2 8.17 us: extended(): lax.ppermute(lax.slice_in_dim(block, 0, width, axis=dim), axis, backward)]
  transfers between devices with their start and end apart: 5 -> 0, of which waited for: 1 -> 0; matrix products, arithmetic and copies ran while one was open for 6% -> 0% of each run, Pallas kernels for 0% -> 0%
where the time goes in v2:
time: 62.7 us; the launch traced here: 62.5 us
  Pallas kernels  58.3 us (93%)
  local copies, waits for them, and re-layouts  3.49 us (6%)
  between operations  0.64 us (1%)
    pallas_call x2, Pallas kernels, call(): pl.pallas_call(kernel, out_shape=outs, in_specs=[VMEM] * len(args), out_s...  58.3 us
    unnamed x5, local copies, waits for them, and re-layouts  3.49 us

profile of v2, /device:TPU:1, one launch (start us, length us, event | category | flops | bytes accessed | tf_op | source)
XLA Modules:
  0.0 62.5 jit_solution(14616755067713866098)
XLA Ops:
  0.6 1.4 %copy.14.refs_4_ = s32[64,16]{1,0:T(8,128)} copy(s32[64,16]{0,1:T(8,128)} %param.15) | data formatting | bytes 8192 | tf_op args[4]
  2.0 0.0 copy-start
  2.0 1.4 %copy.15.refs_5_ = bf16[8,25,25]{2,1,0:T(8,128)(2,1)} copy(bf16[8,25,25]{2,0,1:T(8,128)(2,1)} %param.16) | data formatting | bytes 20000 | tf_op args[5]
  3.5 0.0 copy-done
  3.5 0.6 %copy.16.refs_6_ = bf16[8,25,25]{2,1,0:T(8,128)(2,1)} copy(bf16[8,25,25]{2,0,1:T(8,128)(2,1)S(1)} %copy-done) | data formatting | bytes 20000 | tf_op args[6]
  4.1 56.3 %shard_map.130 = (bf16[128,1024]{1,0:T(8,128)(2,1)}, f32[768,128]{1,0:T(8,128)}) custom-call(bf16[32,1024]{1,0:T(8,128)(2,1)} %charges_ref.1, f32[25,1024]{1,0:T(8,128)} %refs_1_.1, s32[1,1024]{1,0:T(1,128)} %bitcast.1, s32[64,128]{1,0:T(8,128)} %refs_3_.1, s32[64,16]{1,0:T(8,128)} %copy.14.refs_4_, bf16[8,25,25]{2,1,0:T(8,128)(2,1)} %copy.15.refs_5_, ...), custom_call_target="tpu_custom_call" | custom-call | tf_op jit(solution)/shard_map/pallas_call | solution.py:380
  60.4 2.1 %shard_map.131 = (bf16[32,1024]{1,0:T(8,128)(2,1)}, f32[25,25,64]{2,1,0:T(8,128)}, f32[25,25,64]{2,1,0:T(8,128)}) custom-call(bf16[128,1024]{1,0:T(8,128)(2,1)} %get-tuple-element.5.pot_ref, f32[768,128]{1,0:T(8,128)} %get-tuple-element.6.total_ref, bf16[32,1024]{1,0:T(8,128)(2,1)} %charges_ref.1, bf16[128,128]{1,0:T(8,128)(2,1)} %mix_ref.1), custom_call_target="tpu_custom_call" | custom-call | tf_op jit(solution)/shard_map/pallas_call | solution.py:380
Async XLA Ops:
  2.0 1.5 %copy-start = (bf16[8,25,25]{2,0,1:T(8,128)(2,1)S(1)}, bf16[8,25,25]{2,0,1:T(8,128)(2,1)}, u32[]{:S(2)}) copy-start(bf16[8,25,25]{2,0,1:T(8,128)(2,1)} %param.17) | copy-start | bytes 30004

commit v3 on v2

--- a/solution.py
+++ b/solution.py
@@ -119,7 +119,7 @@
     ops[...] = turned[:, 0:KP].astype(BF16)
 
 
-def main_kernel(n_cells, n_chan, n_x, n_z, rc, names, *refs):
+def main_kernel(n_cells, n_chan, n_x, n_z, rc_a, rc_b, names, *refs):
     r = dict(zip(names, refs))
     cells = lax.axis_index("cells")
     chan = lax.axis_index("chan")
@@ -180,10 +180,12 @@
     r["to_right"][...] = jnp.where(low, bottom, top).astype(BF16)
     halo = [send(r["to_left"], r["from_right"], left), send(r["to_right"], r["from_left"], right)]
 
-    for ops_ref, pad in ((r["up"], r["up_pad"]), (r["down"], r["down_pad"])):
+    for ops_ref, pad, rows in ((r["up"], r["up_pad"], r["up_rows"]), (r["down"], r["down_pad"], r["down_rows"])):
         pad[...] = jnp.zeros_like(pad)
+        for i in range(k):
+            rows[i * 8 : (i + 1) * 8, 0:k] = ops_ref[i].astype(F32)
         for o in range(8):
-            pad[o * KP : o * KP + k, 0:k] = ops_ref[o].astype(F32)
+            pad[o * KP : o * KP + k, 0:k] = rows[pl.ds(o, k, stride=8), :][:, 0:k]
     fill_octants(r["octants"])
 
     up_wide = jnp.concatenate([r["up_pad"][o * KP : (o + 1) * KP, :] for o in range(8)], axis=1).astype(BF16)
@@ -194,12 +196,10 @@
     coarse[...] = to_parents(src, r["octants"], up_wide, NN, r["stack"])
     coarse_halo = [send(coarse, r["coarse_right"], left), send(coarse, r["coarse_left"], right)]
 
-    turn_ops(r["leaf_ops"], r["coarse_ops"], r["total"], r["slots"], r["ops"])
-
     raw = r["leaf_lists"][...]
     r["lists"][...] = jnp.where(raw < 0, -1, (raw - cells * LD) & 255)
     raw = r["coarse_lists"][...]
-    raw = jnp.concatenate([raw] * 8, axis=1)
+    raw = jnp.concatenate([raw] * 8, axis=0).T
     at = jnp.where(raw < 0, -1, (raw - cells * CD) & 31)
     c8 = (lane_iota(n_slots, 128) >> 4) * CD
     r["clists"][...] = jnp.where(at < 0, -1, jnp.where(at < CD, c8 + at, 112 + c8 + at))
@@ -225,15 +225,16 @@
             first, r["coarse_right"][:, lanes].astype(F32), r["coarse_left"][:, lanes].astype(F32)
         ).astype(BF16)
 
-    picked, cpicked, slots = r["picked"], r["cpicked"], r["slots"]
-
-    def coarse_group(g, carry):
-        base = pl.multiple_of(g * SG * KP, SG * KP)
-        gather_group(r["clists"], g, csrc, cpicked, base)
-        slots[group_rows(groups + g), 0:KP] = dot(cpicked[group_rows(g), :], r["bfar"][...], NT)
+    picked, cpicked, slots = (r["picked_even"], r["picked_odd"]), r["cpicked"], r["slots"]
+
+    def coarse_group(h, carry):
+        for i in range(2):
+            g = 2 * h + i
+            gather_group(r["clists"], g, csrc, cpicked, pl.multiple_of(g * SG * KP, SG * KP))
         return carry
 
-    lax.fori_loop(0, groups, coarse_group, 0)
+    lax.fori_loop(0, groups // 2, coarse_group, 0)
+    slots[groups * SG * KP : 2 * groups * SG * KP, 0:KP] = dot(cpicked[...], r["bfar"][...], NT)
 
     for copy in halo:
         copy.wait()
@@ -241,47 +242,96 @@
     src[0:512, LD : 2 * LD] = jnp.where(low, a, b).astype(BF16)
     src[512:1024, LD : 2 * LD] = pltpu.roll(jnp.where(low, b, a), 64, 1).astype(BF16)
 
-    def leaf_group(g, carry):
-        base = pl.multiple_of(g * SG * KP, SG * KP)
-        gather_group(r["lists"], g, src, picked, base)
-        slots[group_rows(g), 0:KP] = dot(picked[group_rows(g), :], r["back"][...], NT)
+    def leaf_group(h, carry):
+        for i in range(2):
+            gather_group(r["lists"], 2 * h + i, src, picked[i], pl.multiple_of(h * SG * KP, SG * KP))
+            slots[group_rows(2 * h + i), 0:KP] = dot(picked[i][group_rows(h), :], r["back"][...], NT)
         return carry
 
-    lax.fori_loop(0, groups, leaf_group, 0)
-
-    grad = r["grad"]
-    size = n_plane * rc
-    grad[2 * size - 8 * ((2 * size - k * k) // 8) - 8 :, :] = jnp.zeros(
-        (8 * ((2 * size - k * k) // 8) + 8, 128), F32
-    )
-    for j in range(k):
-        turned = slots[pl.ds(j, 2 * n_slots, stride=KP), :].T
-        grad[pl.ds(j, k, stride=k), :] = turned[0:k, :]
-    half_copy = send(
-        grad.at[pl.ds(pl.multiple_of((1 - core) * size, 8), size), :], r["half_in"], other
-    )
-
-    near, far = r["near"], r["far"]
-    far[...] = jnp.zeros_like(far)
-
-    def far_group(g, carry):
-        far[...] += dot(r["ops"][group_rows(groups + g), :], cpicked[group_rows(g), :], TN)
-        return carry
-
-    lax.fori_loop(0, groups, far_group, 0)
-    half_copy.wait()
-    half = r["half"]
-    half[...] = grad[pl.ds(pl.multiple_of(core * size, 8), size), :] + r["half_in"][...]
-
-    def chunk(d):
-        return pl.ds(pl.multiple_of(d * rc, 8), rc)
-
-    plane_copies = [
-        send(half.at[chunk(d), :], r["part_in"].at[i], device)
-        for i, (d, device) in enumerate(plane_peers)
-    ]
-
-    far16 = far[...].astype(BF16)
+    def pack(grad, first_row, unit):
+        for jb in range(7):
+            turned = jnp.concatenate(
+                [slots[pl.ds(first_row + jb * 4 + i, 32, stride=KP), :] for i in range(4)], axis=0
+            ).T
+            grad[pl.ds(unit * 7 * k + jb, k, stride=7), :] = turned[0:k, :]
+
+    class Exchange:
+        def __init__(self, tag, rc, units):
+            self.refs = {n: r[n + tag] for n in ("grad", "half_in", "half", "part_in", "part", "z_in", "total")}
+            self.rc = rc
+            self.size = n_plane * rc
+            grad = self.refs["grad"]
+            used = 7 * k * len(units) // 8 * 8
+            grad[used:, :] = jnp.zeros((2 * self.size - used, 128), F32)
+            for unit, row in enumerate(units):
+                pack(grad, row, unit)
+            self.core = send(
+                grad.at[pl.ds(pl.multiple_of((1 - core) * self.size, 8), self.size), :],
+                self.refs["half_in"],
+                other,
+            )
+
+        def chunk(self, d):
+            return pl.ds(pl.multiple_of(d * self.rc, 8), self.rc)
+
+        def plane(self):
+            self.core.wait()
+            q = self.refs
+            q["half"][...] = (
+                q["grad"][pl.ds(pl.multiple_of(core * self.size, 8), self.size), :] + q["half_in"][...]
+            )
+            self.copies = [
+                send(q["half"].at[self.chunk(d), :], q["part_in"].at[i], device)
+                for i, (d, device) in enumerate(plane_peers)
+            ]
+
+        def depth(self):
+            q = self.refs
+            for copy in self.copies:
+                copy.wait()
+            summed = q["half"][self.chunk(m), :]
+            for i in range(n_plane - 1):
+                summed = summed + q["part_in"][i]
+            q["part"][...] = summed
+            self.copies = [send(q["part"], q["z_in"].at[z], device) for _, device in z_peers]
+            q["z_in"][z] = summed
+
+        def gather(self):
+            q = self.refs
+            for copy in self.copies:
+                copy.wait()
+            summed = q["z_in"][0]
+            for i in range(1, n_z):
+                summed = summed + q["z_in"][i]
+            own = pl.ds(pl.multiple_of(core * self.size + m * self.rc, 8), self.rc)
+            q["total"][own, :] = summed
+            self.copies = [
+                send(q["total"].at[own, :], q["total"].at[own, :], device) for _, device in plane_peers
+            ]
+
+        def last(self):
+            for copy in self.copies:
+                copy.wait()
+            side = self.refs["total"].at[pl.ds(pl.multiple_of(core * self.size, 8), self.size), :]
+            self.copies = [send(side, side, other)]
+
+        def finish(self):
+            for copy in self.copies:
+                copy.wait()
+
+    halfway = groups * SG * KP // 2
+    lax.fori_loop(0, groups // 4, leaf_group, 0)
+    early = Exchange("_a", rc_a, [2 * halfway, 3 * halfway, 0])
+    lax.fori_loop(groups // 4, 3 * groups // 8, leaf_group, 0)
+    early.plane()
+    lax.fori_loop(3 * groups // 8, groups // 2, leaf_group, 0)
+    late = Exchange("_b", rc_b, [halfway])
+
+    turn_ops(r["leaf_ops"], r["coarse_ops"], r["ops_rows"], r["ops_turned"], r["ops"])
+    late.plane()
+    near = r["near"]
+    far16 = dot(r["ops"][groups * SG * KP : 2 * groups * SG * KP, :], cpicked[...], TN).astype(BF16)
+
     far_rows = jnp.concatenate([far16[:, cb * 128 : (cb + 1) * 128] for cb in range(4)], axis=0)
     octant = lane_iota(KP, 128) & 7
     child = r["child"]
@@ -296,34 +346,20 @@
     for c in range(0, CH * LD, 512):
         near[:, c : c + 512] = dot(down_wide, child[:, c : c + 512])
 
-    def near_group(g, carry):
-        ops = r["ops"][group_rows(g), :]
+    def near_group(h, carry):
+        even, odd = r["ops"][group_rows(2 * h), :], r["ops"][group_rows(2 * h + 1), :]
         for c in range(0, CH * LD, 512):
-            near[:, c : c + 512] += dot(ops, picked[group_rows(g), c : c + 512], TN)
+            lanes = slice(c, c + 512)
+            near[:, lanes] += dot(even, picked[0][group_rows(h), lanes], TN) + dot(
+                odd, picked[1][group_rows(h), lanes], TN
+            )
         return carry
 
-    lax.fori_loop(0, groups // 2, near_group, 0)
-
-    for copy in plane_copies:
-        copy.wait()
-    summed = half[chunk(m), :]
-    for i in range(n_plane - 1):
-        summed = summed + r["part_in"][i]
-    r["part"][...] = summed
-    z_copies = [send(r["part"], r["z_in"].at[z], device) for _, device in z_peers]
-    r["z_in"][z] = summed
-
-    lax.fori_loop(groups // 2, groups, near_group, 0)
-
-    for copy in z_copies:
-        copy.wait()
-    summed = r["z_in"][0]
-    for i in range(1, n_z):
-        summed = summed + r["z_in"][i]
-    total = r["total_out"]
-    own = pl.ds(pl.multiple_of(core * size + m * rc, 8), rc)
-    total[own, :] = summed
-    gather_copies = [send(total.at[own, :], total.at[own, :], device) for _, device in plane_peers]
+    lax.fori_loop(0, 1, near_group, 0)
+    early.depth()
+    lax.fori_loop(1, 3, near_group, 0)
+    late.depth()
+    lax.fori_loop(3, groups // 2, near_group, 0)
 
     expand = bexp
     for c in range(CH):
@@ -349,31 +385,45 @@
     pot_copies = [send(pot, pot_all.at[mine, :], d) for d in chan_peers]
     pot_all[mine, :] = pot[...]
 
-    for copy in gather_copies:
-        copy.wait()
-    side = pl.ds(pl.multiple_of(core * size, 8), size)
-    last = send(total.at[side, :], total.at[side, :], other)
+    r["mixt"][...] = r["mix"][...].astype(F32).T.astype(BF16)
+    early.gather()
+    late.gather()
     for copy in pot_copies:
         copy.wait()
-    last.wait()
-
-
-def final_kernel(pot_ref, total_ref, charges_ref, mix_ref, out_ref, gl_ref, gc_ref, mixt):
-    chan = lax.axis_index("chan")
-    k, _, slots = gl_ref.shape
-    mixt[...] = mix_ref[...].astype(F32).T.astype(BF16)
-    mine = pl.ds(pl.multiple_of(chan * CH, CH), CH)
-    out_ref[...] = (charges_ref[...].astype(F32) + dot(mixt[mine, :], pot_ref[...])).astype(BF16)
+    r["refined"][...] = (
+        r["charges"][...].astype(F32) + dot(r["mixt"][mine, :], pot_all[...])
+    ).astype(BF16)
+    early.last()
+    late.last()
+    early.finish()
+    late.finish()
+
+
+def final_kernel(refined_ref, early_ref, late_ref, out_ref, gl_ref, gc_ref):
+    k = gl_ref.shape[0]
+    out_ref[...] = refined_ref[...]
+    unit = 7 * k
+
+    def rows(ref, u, i):
+        return ref[u * unit + i * 7 : u * unit + (i + 1) * 7, :]
+
     for i in range(k):
-        block = total_ref[i * k : (i + 1) * k, :]
-        gl_ref[i] = block[:, 0:slots]
-        gc_ref[i] = pltpu.roll(block, 128 - slots, 1)[:, 0:slots]
+        for out, low, high in (
+            (gc_ref, rows(early_ref, 0, i), rows(early_ref, 1, i)),
+            (gl_ref, rows(early_ref, 2, i), rows(late_ref, 0, i)),
+        ):
+            for j in range(4):
+                count = 7 if j == 0 else 6
+                both = jnp.concatenate(
+                    [low[0:count, j * 32 : (j + 1) * 32], high[0:count, j * 32 : (j + 1) * 32]], axis=1
+                )
+                out[i, pl.ds(j, count, stride=4), :] = both
 
 
 VMEM = pl.BlockSpec(memory_space=pltpu.VMEM)
 
 
-def call(kernel, outs, scratch, args, collective=None):
+def call(kernel, outs, scratch, args, mib, collective=None):
     extra = {}
     if collective is not None:
         extra = dict(collective_id=collective, has_side_effects=True)
@@ -383,7 +433,7 @@
         in_specs=[VMEM] * len(args),
         out_specs=[VMEM] * len(outs),
         scratch_shapes=scratch,
-        compiler_params=pltpu.CompilerParams(vmem_limit_bytes=60 << 20, **extra),
+        compiler_params=pltpu.CompilerParams(vmem_limit_bytes=mib << 20, **extra),
     )(*args)
 
 
@@ -393,17 +443,18 @@
     slots = leaf_lists.shape[0]
     shape = jax.ShapeDtypeStruct
     n_plane = n_x * n_chan
-    rc = -(-k * k // (16 * n_plane)) * 8
+    rc_a, rc_b = (-(-units * 7 * k // (16 * n_plane)) * 8 for units in (3, 1))
     args = dict(
         charges=charges, basis=basis, leaf=atom_leaf.reshape(1, atoms), leaf_lists=leaf_lists,
-        coarse_lists=coarse_lists, up=up_ops, down=down_ops, leaf_ops=leaf_ops, coarse_ops=coarse_ops,
+        coarse_lists=coarse_lists.T, up=jnp.transpose(up_ops, (1, 0, 2)), down=jnp.transpose(down_ops, (1, 0, 2)), leaf_ops=leaf_ops, coarse_ops=coarse_ops,
         mix=mix, cot=cotangent,
     )
     outs = dict(
-        pot_all=shape((n_chan * CH, atoms), BF16),
-        total_out=shape((2 * n_plane * rc, 128), F32),
-    )
-    copies = 2 * (n_chan - 1) + 4 + 2 + 2 * (n_plane - 1) + n_z - 1
+        refined=shape((CH, atoms), BF16),
+        total_a=shape((2 * n_plane * rc_a, 128), F32),
+        total_b=shape((2 * n_plane * rc_b, 128), F32),
+    )
+    copies = 2 * (n_chan - 1) + 4 + 2 * (2 + 2 * (n_plane - 1) + n_z - 1)
     scratch = dict(
         cot_all=((n_chan * CH, atoms), BF16),
         basis_pad=((KP, atoms), F32),
@@ -427,35 +478,43 @@
         down_pad=((8 * KP, KP), F32),
         lists=((slots, LD), jnp.int32),
         clists=((slots, 128), jnp.int32),
-        picked=((slots * KP, CH * LD), BF16),
+        picked_even=((slots * KP // 2, CH * LD), BF16),
+        picked_odd=((slots * KP // 2, CH * LD), BF16),
         cpicked=((slots * KP, CH * CD), BF16),
         child=((8 * KP, CH * LD), BF16),
         near=((KP, CH * LD), F32),
-        far=((KP, CH * CD), F32),
-        total=((KP * KP, 128), F32),
+        up_rows=((8 * k, 128), F32),
+        down_rows=((8 * k, 128), F32),
+        pot_all=((n_chan * CH, atoms), BF16),
+        mixt=(mix.shape, BF16),
+        ops_rows=((KP * KP, 128), F32),
+        ops_turned=((2 * slots * KP, 128), F32),
         slots=((2 * slots * KP, 128), F32),
         ops=((2 * slots * KP, KP), BF16),
-        grad=((2 * n_plane * rc, 128), F32),
-        half_in=((n_plane * rc, 128), F32),
-        half=((n_plane * rc, 128), F32),
-        part_in=((n_plane - 1, rc, 128), F32),
-        part=((rc, 128), F32),
-        z_in=((n_z, rc, 128), F32),
         pot=((CH, atoms), BF16),
     )
+    for tag, rc in (("_a", rc_a), ("_b", rc_b)):
+        scratch["grad" + tag] = ((2 * n_plane * rc, 128), F32)
+        scratch["half_in" + tag] = ((n_plane * rc, 128), F32)
+        scratch["half" + tag] = ((n_plane * rc, 128), F32)
+        scratch["part_in" + tag] = ((n_plane - 1, rc, 128), F32)
+        scratch["part" + tag] = ((rc, 128), F32)
+        scratch["z_in" + tag] = ((n_z, rc, 128), F32)
     names = tuple(args) + tuple(outs) + tuple(scratch) + ("sends", "recvs")
-    pot_all, total = call(
-        functools.partial(main_kernel, n_cells, n_chan, n_x, n_z, rc, names),
+    refined, early, late = call(
+        functools.partial(main_kernel, n_cells, n_chan, n_x, n_z, rc_a, rc_b, names),
         list(outs.values()),
         [pltpu.VMEM(*v) for v in scratch.values()] + [pltpu.SemaphoreType.DMA((copies,))] * 2,
         tuple(args.values()),
+        40,
         collective=0,
     )
     return call(
         final_kernel,
         [shape((CH, atoms), BF16), shape((k, k, slots), F32), shape((k, k, slots), F32)],
-        [pltpu.VMEM(mix.shape, BF16)],
-        (pot_all, total, charges, mix),
+        [],
+        (refined, early, late),
+        8,
     )
 
 

time: 62.7 us -> 65.4 us (1.043)
  local copies, waits for them, and re-layouts: 3.49 us -> 8.94 us
  Pallas kernels: 58.3 us -> 55.2 us
    unnamed x5 -> x22, local copies, waits for them, and re-layouts: 3.49 us -> 8.94 us
    pallas_call x2, Pallas kernels: 58.3 us -> 55.2 us  [call(): pl.pallas_call(kernel, out_shape=outs, in_specs=[VMEM] * len(args), out_s...]
where the time goes in v3:
time: 65.4 us; the launch traced here: 64.8 us
  Pallas kernels  55.2 us (84%)
  local copies, waits for them, and re-layouts  8.94 us (14%)
  between operations  0.66 us (1%)
    pallas_call x2, Pallas kernels, call(): pl.pallas_call(kernel, out_shape=outs, in_specs=[VMEM] * len(args), out_s...  55.2 us
    unnamed x22, local copies, waits for them, and re-layouts  8.94 us

profile of v3, /device:TPU:1, one launch (start us, length us, event | category | flops | bytes accessed | tf_op | source)
XLA Modules:
  0.0 64.8 jit_solution(1156130938223795587)
XLA Ops:
  0.6 0.0 copy-start.10
  0.6 0.7 %copy-done.10 = s32[1024]{0:T(1024)S(1)} copy-done((s32[1024]{0:T(1024)S(1)}, s32[1024]{0:T(1024)}, u32[]{:S(2)}) %copy-start.10) | copy-done | bytes 4120
  1.3 0.0 copy-start
  1.3 0.9 %copy-done = bf16[25,25,64]{2,1,0:T(8,128)(2,1)S(1)} copy-done((bf16[25,25,64]{2,1,0:T(8,128)(2,1)S(1)}, bf16[25,25,64]{2,1,0:T(8,128)(2,1)}, u32[]{:S(2)}) %copy-start) | copy-done | bytes 80024
  2.3 0.0 copy-start.1
  2.3 0.9 %copy-done.1 = bf16[25,25,64]{2,1,0:T(8,128)(2,1)S(1)} copy-done((bf16[25,25,64]{2,1,0:T(8,128)(2,1)S(1)}, bf16[25,25,64]{2,1,0:T(8,128)(2,1)}, u32[]{:S(2)}) %copy-start.1) | copy-done | bytes 80024
  3.2 0.0 copy-start.2
  3.2 0.9 %copy-done.2 = f32[25,1024]{1,0:T(8,128)S(1)} copy-done((f32[25,1024]{1,0:T(8,128)S(1)}, f32[25,1024]{1,0:T(8,128)}, u32[]{:S(2)}) %copy-start.2) | copy-done | bytes 102424
  4.1 0.0 copy-start.3
  4.1 0.8 %copy-done.3 = bf16[32,1024]{1,0:T(8,128)(2,1)S(1)} copy-done((bf16[32,1024]{1,0:T(8,128)(2,1)S(1)}, bf16[32,1024]{1,0:T(8,128)(2,1)}, u32[]{:S(2)}) %copy-start.3) | copy-done | bytes 65560
  4.9 0.0 copy-start.4
  4.9 0.8 %copy-done.4 = bf16[32,1024]{1,0:T(8,128)(2,1)S(1)} copy-done((bf16[32,1024]{1,0:T(8,128)(2,1)S(1)}, bf16[32,1024]{1,0:T(8,128)(2,1)}, u32[]{:S(2)}) %copy-start.4) | copy-done | bytes 65560
  5.8 0.0 copy-start.5
  5.8 0.8 %copy-done.5 = bf16[8,25,25]{2,0,1:T(8,128)(2,1)S(1)} copy-done((bf16[8,25,25]{2,0,1:T(8,128)(2,1)S(1)}, bf16[8,25,25]{2,0,1:T(8,128)(2,1)}, u32[]{:S(2)}) %copy-start.5) | copy-done | bytes 10024
  6.6 0.0 copy-start.6
  6.6 0.8 %copy-done.6 = bf16[8,25,25]{2,0,1:T(8,128)(2,1)S(1)} copy-done((bf16[8,25,25]{2,0,1:T(8,128)(2,1)S(1)}, bf16[8,25,25]{2,0,1:T(8,128)(2,1)}, u32[]{:S(2)}) %copy-start.6) | copy-done | bytes 10024
  7.4 0.0 copy-start.7
  7.4 0.8 %copy-done.7 = s32[64,128]{1,0:T(8,128)S(1)} copy-done((s32[64,128]{1,0:T(8,128)S(1)}, s32[64,128]{1,0:T(8,128)}, u32[]{:S(2)}) %copy-start.7) | copy-done | bytes 32792
  8.1 0.0 copy-start.8
  8.1 0.8 %copy-done.8 = bf16[128,128]{1,0:T(8,128)(2,1)S(1)} copy-done((bf16[128,128]{1,0:T(8,128)(2,1)S(1)}, bf16[128,128]{1,0:T(8,128)(2,1)}, u32[]{:S(2)}) %copy-start.8) | copy-done | bytes 32792
  8.9 0.0 copy-start.9
  8.9 0.7 %copy-done.9 = s32[64,16]{0,1:T(8,128)S(1)} copy-done((s32[64,16]{0,1:T(8,128)S(1)}, s32[64,16]{0,1:T(8,128)}, u32[]{:S(2)}) %copy-start.9) | copy-done | bytes 4120
  9.6 54.0 %shard_map.130 = (bf16[32,1024]{1,0:T(8,128)(2,1)S(1)}, f32[768,128]{1,0:T(8,128)S(1)}, f32[256,128]{1,0:T(8,128)S(1)}) custom-call(bf16[32,1024]{1,0:T(8,128)(2,1)S(1)} %copy-done.3, f32[25,1024]{1,0:T(8,128)S(1)} %copy-done.2, s32[1,1024]{1,0:T(1,128)S(1)} %bitcast.7, s32[64,128]{1,0:T(8,128)S(1)} %copy-done.7, s32[16,64]{1,0:T(8,128)S(1)} %bitcast.6, ...), custom_call_target="tpu_custom_call" | custom-call | tf_op jit(solution)/shard_map/pallas_call | solution.py:430
  63.6 1.3 %shard_map.131 = (bf16[32,1024]{1,0:T(8,128)(2,1)}, f32[25,25,64]{2,1,0:T(8,128)}, f32[25,25,64]{2,1,0:T(8,128)}) custom-call(bf16[32,1024]{1,0:T(8,128)(2,1)S(1)} %get-tuple-element.6.refined_ref, f32[768,128]{1,0:T(8,128)S(1)} %get-tuple-element.7.early_ref, f32[256,128]{1,0:T(8,128)S(1)} %get-tuple-element.8.late_ref), custom_call_target="tpu_custom_call" | custom-call | tf_op jit(solution)/shard_map/pallas_call | solution.py:430
Async XLA Ops:
  0.6 0.7 %copy-start.10 = (s32[1024]{0:T(1024)S(1)}, s32[1024]{0:T(1024)}, u32[]{:S(2)}) copy-start(s32[1024]{0:T(1024)} %param.13) | copy-start | bytes 12292
  1.3 0.9 %copy-start = (bf16[25,25,64]{2,1,0:T(8,128)(2,1)S(1)}, bf16[25,25,64]{2,1,0:T(8,128)(2,1)}, u32[]{:S(2)}) copy-start(bf16[25,25,64]{2,1,0:T(8,128)(2,1)} %refs_7_.1) | copy-start | bytes 240004
  2.3 0.9 %copy-start.1 = (bf16[25,25,64]{2,1,0:T(8,128)(2,1)S(1)}, bf16[25,25,64]{2,1,0:T(8,128)(2,1)}, u32[]{:S(2)}) copy-start(bf16[25,25,64]{2,1,0:T(8,128)(2,1)} %refs_8_.1) | copy-start | bytes 240004
  3.2 0.9 %copy-start.2 = (f32[25,1024]{1,0:T(8,128)S(1)}, f32[25,1024]{1,0:T(8,128)}, u32[]{:S(2)}) copy-start(f32[25,1024]{1,0:T(8,128)} %refs_1_.1) | copy-start | bytes 307204
  4.1 0.8 %copy-start.3 = (bf16[32,1024]{1,0:T(8,128)(2,1)S(1)}, bf16[32,1024]{1,0:T(8,128)(2,1)}, u32[]{:S(2)}) copy-start(bf16[32,1024]{1,0:T(8,128)(2,1)} %refs_0_.1) | copy-start | bytes 196612
  4.9 0.8 %copy-start.4 = (bf16[32,1024]{1,0:T(8,128)(2,1)S(1)}, bf16[32,1024]{1,0:T(8,128)(2,1)}, u32[]{:S(2)}) copy-start(bf16[32,1024]{1,0:T(8,128)(2,1)} %refs_10_.1) | copy-start | bytes 196612
  5.8 0.8 %copy-start.5 = (bf16[8,25,25]{2,0,1:T(8,128)(2,1)S(1)}, bf16[8,25,25]{2,0,1:T(8,128)(2,1)}, u32[]{:S(2)}) copy-start(bf16[8,25,25]{2,0,1:T(8,128)(2,1)} %param.16) | copy-start | bytes 30004
  6.6 0.8 %copy-start.6 = (bf16[8,25,25]{2,0,1:T(8,128)(2,1)S(1)}, bf16[8,25,25]{2,0,1:T(8,128)(2,1)}, u32[]{:S(2)}) copy-start(bf16[8,25,25]{2,0,1:T(8,128)(2,1)} %param.17) | copy-start | bytes 30004
  7.4 0.8 %copy-start.7 = (s32[64,128]{1,0:T(8,128)S(1)}, s32[64,128]{1,0:T(8,128)}, u32[]{:S(2)}) copy-start(s32[64,128]{1,0:T(8,128)} %refs_3_.1) | copy-start | bytes 98308
  8.1 0.8 %copy-start.8 = (bf16[128,128]{1,0:T(8,128)(2,1)S(1)}, bf16[128,128]{1,0:T(8,128)(2,1)}, u32[]{:S(2)}) copy-start(bf16[128,128]{1,0:T(8,128)(2,1)} %refs_9_.1) | copy-start | bytes 98308
  8.9 0.7 %copy-start.9 = (s32[64,16]{0,1:T(8,128)S(1)}, s32[64,16]{0,1:T(8,128)}, u32[]{:S(2)}) copy-start(s32[64,16]{0,1:T(8,128)} %param.15) | copy-start | bytes 12292

commit v4 on v2

--- a/solution.py
+++ b/solution.py
@@ -10,6 +10,7 @@
 MESH = pl.DeviceIdType.MESH
 BF16 = jnp.bfloat16
 F32 = jnp.float32
+ARGS = ("leaf", "basis", "charges", "cot", "up", "down", "leaf_lists", "coarse_lists", "leaf_ops", "coarse_ops", "mix")
 KP = 32
 CH = 32
 LD = 128
@@ -126,27 +127,42 @@
     core = lax.rem(cells, 2)
     x = lax.rem(cells // 2, n_x)
     z = cells // (2 * n_x)
-    n_plane = n_x * n_chan
-    m = x * n_chan + chan
-    k = r["basis"].shape[0]
-    n_slots = r["leaf_lists"].shape[0]
+    n_plane = 2 * n_x * n_chan
+    m = (x * n_chan + chan) * 2 + core
+    k = r["basis_hbm"].shape[0]
+    n_slots = r["leaf_lists_hbm"].shape[0]
     groups = n_slots // SG
     left = (lax.rem(cells + n_cells - 1, n_cells), chan)
     right = (lax.rem(cells + 1, n_cells), chan)
-    other = (cells + 1 - 2 * core, chan)
     chan_peers = [(cells, lax.rem(chan + i, n_chan)) for i in range(1, n_chan)]
     plane_peers, z_peers = [], []
     for i in range(1, n_plane):
         d = lax.rem(m + i, n_plane)
-        plane_peers.append((d, ((z * n_x + d // n_chan) * 2 + core, lax.rem(d, n_chan))))
+        place = d // 2
+        plane_peers.append(
+            (d, ((z * n_x + place // n_chan) * 2 + lax.rem(d, 2), lax.rem(place, n_chan)))
+        )
     for i in range(1, n_z):
         d = lax.rem(z + i, n_z)
         z_peers.append((d, ((d * n_x + x) * 2 + core, chan)))
 
     barrier = pltpu.get_barrier_semaphore()
-    greeted = chan_peers + [left, right, other] + [d for _, d in plane_peers] + [d for _, d in z_peers]
+    greeted = chan_peers + [left, right] + [d for _, d in plane_peers] + [d for _, d in z_peers]
     for device in greeted:
         pl.semaphore_signal(barrier, inc=1, device_id=device, device_id_type=MESH)
+
+    pending = {}
+    for i, name in enumerate(ARGS):
+        if name == "cot":
+            target = r["cot_all"].at[pl.ds(pl.multiple_of(chan * CH, CH), CH), :]
+        else:
+            target = r[name]
+        pending[name] = pltpu.make_async_copy(r[name + "_hbm"], target, r["loads"].at[i])
+        pending[name].start()
+
+    def load(*names):
+        for name in names:
+            pending.pop(name).wait()
 
     sems = {"next": 0}
 
@@ -165,13 +181,15 @@
         return copy
 
     member, basis_pad, src, bexp = r["member"], r["basis_pad"], r["src"], r["bexp"]
+    load("leaf", "basis")
     fill_member(r["leaf"], member, cells * LD)
     fill_basis(r["basis"], basis_pad)
     pl.semaphore_wait(barrier, len(greeted))
 
     mine = pl.ds(pl.multiple_of(chan * CH, CH), CH)
-    cot_copies = [send(r["cot"], r["cot_all"].at[mine, :], d) for d in chan_peers]
-
+    cot_copies = [send(r["cot_hbm"], r["cot_all"].at[mine, :], d) for d in chan_peers]
+
+    load("charges")
     spread(r["charges"], basis_pad, member, src)
     low = lane_iota(512, 128) < 64
     top = src[0:512, 0:LD].astype(F32)
@@ -180,10 +198,13 @@
     r["to_right"][...] = jnp.where(low, bottom, top).astype(BF16)
     halo = [send(r["to_left"], r["from_right"], left), send(r["to_right"], r["from_left"], right)]
 
-    for ops_ref, pad in ((r["up"], r["up_pad"]), (r["down"], r["down_pad"])):
+    load("up", "down")
+    for ops_ref, pad, rows in ((r["up"], r["up_pad"], r["up_rows"]), (r["down"], r["down_pad"], r["down_rows"])):
         pad[...] = jnp.zeros_like(pad)
+        for i in range(k):
+            rows[i * 8 : (i + 1) * 8, 0:k] = ops_ref[i].astype(F32)
         for o in range(8):
-            pad[o * KP : o * KP + k, 0:k] = ops_ref[o].astype(F32)
+            pad[o * KP : o * KP + k, 0:k] = rows[pl.ds(o, k, stride=8), :][:, 0:k]
     fill_octants(r["octants"])
 
     up_wide = jnp.concatenate([r["up_pad"][o * KP : (o + 1) * KP, :] for o in range(8)], axis=1).astype(BF16)
@@ -194,24 +215,42 @@
     coarse[...] = to_parents(src, r["octants"], up_wide, NN, r["stack"])
     coarse_halo = [send(coarse, r["coarse_right"], left), send(coarse, r["coarse_left"], right)]
 
-    turn_ops(r["leaf_ops"], r["coarse_ops"], r["total"], r["slots"], r["ops"])
-
+    load("leaf_lists", "coarse_lists", "leaf_ops", "coarse_ops", "mix", "cot")
     raw = r["leaf_lists"][...]
     r["lists"][...] = jnp.where(raw < 0, -1, (raw - cells * LD) & 255)
     raw = r["coarse_lists"][...]
-    raw = jnp.concatenate([raw] * 8, axis=1)
+    raw = jnp.concatenate([raw] * 8, axis=0).T
     at = jnp.where(raw < 0, -1, (raw - cells * CD) & 31)
     c8 = (lane_iota(n_slots, 128) >> 4) * CD
     r["clists"][...] = jnp.where(at < 0, -1, jnp.where(at < CD, c8 + at, 112 + c8 + at))
 
-    r["cot_all"][mine, :] = r["cot"][...]
+    turn_ops(r["leaf_ops"], r["coarse_ops"], r["ops_rows"], r["ops_turned"], r["ops"])
+    r["mixt"][...] = r["mix"][...].astype(F32).T.astype(BF16)
+
+    for copy in halo:
+        copy.wait()
+    a, b = r["from_right"][...].astype(F32), r["from_left"][...].astype(F32)
+    src[0:512, LD : 2 * LD] = jnp.where(low, a, b).astype(BF16)
+    src[512:1024, LD : 2 * LD] = pltpu.roll(jnp.where(low, b, a), 64, 1).astype(BF16)
+    picked, cpicked, slots = r["picked"], r["cpicked"], r["slots"]
+
+    def leaf_gather(g, carry):
+        gather_group(r["lists"], g, src, picked, pl.multiple_of(g * SG * KP, SG * KP))
+        return carry
+
+    def leaf_gradient(g, carry):
+        slots[group_rows(g), 0:KP] = dot(picked[group_rows(g), :], r["back"][...], NT)
+        return carry
+
+    lax.fori_loop(0, 2, leaf_gather, 0)
+
     for copy in cot_copies:
         copy.wait()
     r["back_pot"][...] = dot(r["mix"][mine, :], r["cot_all"][...]).astype(BF16)
     spread(r["back_pot"], basis_pad, member, bexp)
-    r["bfar"][...] = to_parents(bexp, r["octants"], down_tall, TN, r["stack"])
     for c in range(CH):
         r["back"][:, c * LD : (c + 1) * LD] = bexp[c * KP : (c + 1) * KP, :]
+    r["bfar"][...] = to_parents(bexp, r["octants"], down_tall, TN, r["stack"])
 
     for copy in coarse_halo:
         copy.wait()
@@ -225,63 +264,39 @@
             first, r["coarse_right"][:, lanes].astype(F32), r["coarse_left"][:, lanes].astype(F32)
         ).astype(BF16)
 
-    picked, cpicked, slots = r["picked"], r["cpicked"], r["slots"]
-
-    def coarse_group(g, carry):
-        base = pl.multiple_of(g * SG * KP, SG * KP)
-        gather_group(r["clists"], g, csrc, cpicked, base)
-        slots[group_rows(groups + g), 0:KP] = dot(cpicked[group_rows(g), :], r["bfar"][...], NT)
+    def coarse_group(h, carry):
+        for i in range(2):
+            g = 2 * h + i
+            gather_group(r["clists"], g, csrc, cpicked, pl.multiple_of(g * SG * KP, SG * KP))
         return carry
 
-    lax.fori_loop(0, groups, coarse_group, 0)
-
-    for copy in halo:
-        copy.wait()
-    a, b = r["from_right"][...].astype(F32), r["from_left"][...].astype(F32)
-    src[0:512, LD : 2 * LD] = jnp.where(low, a, b).astype(BF16)
-    src[512:1024, LD : 2 * LD] = pltpu.roll(jnp.where(low, b, a), 64, 1).astype(BF16)
+    lax.fori_loop(0, groups // 2, coarse_group, 0)
+    slots[groups * SG * KP : 2 * groups * SG * KP, 0:KP] = dot(cpicked[...], r["bfar"][...], NT)
 
     def leaf_group(g, carry):
-        base = pl.multiple_of(g * SG * KP, SG * KP)
-        gather_group(r["lists"], g, src, picked, base)
-        slots[group_rows(g), 0:KP] = dot(picked[group_rows(g), :], r["back"][...], NT)
-        return carry
-
-    lax.fori_loop(0, groups, leaf_group, 0)
-
-    grad = r["grad"]
-    size = n_plane * rc
-    grad[2 * size - 8 * ((2 * size - k * k) // 8) - 8 :, :] = jnp.zeros(
-        (8 * ((2 * size - k * k) // 8) + 8, 128), F32
-    )
+        leaf_gather(g, 0)
+        return leaf_gradient(g, 0)
+
+    lax.fori_loop(0, 2, leaf_gradient, 0)
+    lax.fori_loop(2, groups, leaf_group, 0)
+
+    grad, part_in, z_in, total = r["grad"], r["part_in"], r["z_in"], r["total"]
+    used = k * k // 8 * 8
+    grad[used:, :] = jnp.zeros((n_plane * rc - used, 128), F32)
     for j in range(k):
         turned = slots[pl.ds(j, 2 * n_slots, stride=KP), :].T
         grad[pl.ds(j, k, stride=k), :] = turned[0:k, :]
-    half_copy = send(
-        grad.at[pl.ds(pl.multiple_of((1 - core) * size, 8), size), :], r["half_in"], other
-    )
-
-    near, far = r["near"], r["far"]
-    far[...] = jnp.zeros_like(far)
-
-    def far_group(g, carry):
-        far[...] += dot(r["ops"][group_rows(groups + g), :], cpicked[group_rows(g), :], TN)
-        return carry
-
-    lax.fori_loop(0, groups, far_group, 0)
-    half_copy.wait()
-    half = r["half"]
-    half[...] = grad[pl.ds(pl.multiple_of(core * size, 8), size), :] + r["half_in"][...]
 
     def chunk(d):
         return pl.ds(pl.multiple_of(d * rc, 8), rc)
 
     plane_copies = [
-        send(half.at[chunk(d), :], r["part_in"].at[i], device)
-        for i, (d, device) in enumerate(plane_peers)
+        send(grad.at[chunk(d), :], part_in.at[i], device) for i, (d, device) in enumerate(plane_peers)
     ]
 
-    far16 = far[...].astype(BF16)
+    near = r["near"]
+    far16 = dot(r["ops"][groups * SG * KP : 2 * groups * SG * KP, :], cpicked[...], TN).astype(BF16)
+
     far_rows = jnp.concatenate([far16[:, cb * 128 : (cb + 1) * 128] for cb in range(4)], axis=0)
     octant = lane_iota(KP, 128) & 7
     child = r["child"]
@@ -302,28 +317,16 @@
             near[:, c : c + 512] += dot(ops, picked[group_rows(g), c : c + 512], TN)
         return carry
 
-    lax.fori_loop(0, groups // 2, near_group, 0)
-
+    lax.fori_loop(0, 6, near_group, 0)
     for copy in plane_copies:
         copy.wait()
-    summed = half[chunk(m), :]
+    summed = grad[chunk(m), :]
     for i in range(n_plane - 1):
-        summed = summed + r["part_in"][i]
+        summed = summed + part_in[i]
     r["part"][...] = summed
-    z_copies = [send(r["part"], r["z_in"].at[z], device) for _, device in z_peers]
-    r["z_in"][z] = summed
-
-    lax.fori_loop(groups // 2, groups, near_group, 0)
-
-    for copy in z_copies:
-        copy.wait()
-    summed = r["z_in"][0]
-    for i in range(1, n_z):
-        summed = summed + r["z_in"][i]
-    total = r["total_out"]
-    own = pl.ds(pl.multiple_of(core * size + m * rc, 8), rc)
-    total[own, :] = summed
-    gather_copies = [send(total.at[own, :], total.at[own, :], device) for _, device in plane_peers]
+    z_copies = [send(r["part"], z_in.at[z], device) for _, device in z_peers]
+    z_in[z] = summed
+    lax.fori_loop(6, groups, near_group, 0)
 
     expand = bexp
     for c in range(CH):
@@ -349,21 +352,26 @@
     pot_copies = [send(pot, pot_all.at[mine, :], d) for d in chan_peers]
     pot_all[mine, :] = pot[...]
 
+    for copy in z_copies:
+        copy.wait()
+    summed = z_in[0]
+    for i in range(1, n_z):
+        summed = summed + z_in[i]
+    total[chunk(m), :] = summed
+    gather_copies = [send(total.at[chunk(m), :], total.at[chunk(m), :], device) for _, device in plane_peers]
+
+    for copy in pot_copies:
+        copy.wait()
+    r["refined"][...] = (
+        r["charges"][...].astype(F32) + dot(r["mixt"][mine, :], pot_all[...])
+    ).astype(BF16)
     for copy in gather_copies:
         copy.wait()
-    side = pl.ds(pl.multiple_of(core * size, 8), size)
-    last = send(total.at[side, :], total.at[side, :], other)
-    for copy in pot_copies:
-        copy.wait()
-    last.wait()
-
-
-def final_kernel(pot_ref, total_ref, charges_ref, mix_ref, out_ref, gl_ref, gc_ref, mixt):
-    chan = lax.axis_index("chan")
+
+
+def final_kernel(refined_ref, total_ref, out_ref, gl_ref, gc_ref):
     k, _, slots = gl_ref.shape
-    mixt[...] = mix_ref[...].astype(F32).T.astype(BF16)
-    mine = pl.ds(pl.multiple_of(chan * CH, CH), CH)
-    out_ref[...] = (charges_ref[...].astype(F32) + dot(mixt[mine, :], pot_ref[...])).astype(BF16)
+    out_ref[...] = refined_ref[...]
     for i in range(k):
         block = total_ref[i * k : (i + 1) * k, :]
         gl_ref[i] = block[:, 0:slots]
@@ -371,19 +379,20 @@
 
 
 VMEM = pl.BlockSpec(memory_space=pltpu.VMEM)
-
-
-def call(kernel, outs, scratch, args, collective=None):
+HBM = pl.BlockSpec(memory_space=pltpu.HBM)
+
+
+def call(kernel, outs, scratch, args, mib, space, collective=None):
     extra = {}
     if collective is not None:
         extra = dict(collective_id=collective, has_side_effects=True)
     return pl.pallas_call(
         kernel,
         out_shape=outs,
-        in_specs=[VMEM] * len(args),
+        in_specs=[space] * len(args),
         out_specs=[VMEM] * len(outs),
         scratch_shapes=scratch,
-        compiler_params=pltpu.CompilerParams(vmem_limit_bytes=60 << 20, **extra),
+        compiler_params=pltpu.CompilerParams(vmem_limit_bytes=mib << 20, **extra),
     )(*args)
 
 
@@ -392,18 +401,18 @@
     k, atoms = basis.shape
     slots = leaf_lists.shape[0]
     shape = jax.ShapeDtypeStruct
-    n_plane = n_x * n_chan
-    rc = -(-k * k // (16 * n_plane)) * 8
+    n_plane = 2 * n_x * n_chan
+    rc = -(-k * k // (8 * n_plane)) * 8
     args = dict(
         charges=charges, basis=basis, leaf=atom_leaf.reshape(1, atoms), leaf_lists=leaf_lists,
-        coarse_lists=coarse_lists, up=up_ops, down=down_ops, leaf_ops=leaf_ops, coarse_ops=coarse_ops,
+        coarse_lists=coarse_lists.T, up=jnp.transpose(up_ops, (1, 0, 2)), down=jnp.transpose(down_ops, (1, 0, 2)), leaf_ops=leaf_ops, coarse_ops=coarse_ops,
         mix=mix, cot=cotangent,
     )
     outs = dict(
-        pot_all=shape((n_chan * CH, atoms), BF16),
-        total_out=shape((2 * n_plane * rc, 128), F32),
-    )
-    copies = 2 * (n_chan - 1) + 4 + 2 + 2 * (n_plane - 1) + n_z - 1
+        refined=shape((CH, atoms), BF16),
+        total=shape((n_plane * rc, 128), F32),
+    )
+    copies = 2 * (n_chan - 1) + 4 + 2 * (n_plane - 1) + n_z - 1
     scratch = dict(
         cot_all=((n_chan * CH, atoms), BF16),
         basis_pad=((KP, atoms), F32),
@@ -431,31 +440,41 @@
         cpicked=((slots * KP, CH * CD), BF16),
         child=((8 * KP, CH * LD), BF16),
         near=((KP, CH * LD), F32),
-        far=((KP, CH * CD), F32),
-        total=((KP * KP, 128), F32),
+        up_rows=((8 * k, 128), F32),
+        down_rows=((8 * k, 128), F32),
+        pot_all=((n_chan * CH, atoms), BF16),
+        mixt=(mix.shape, BF16),
+        ops_rows=((KP * KP, 128), F32),
+        ops_turned=((2 * slots * KP, 128), F32),
         slots=((2 * slots * KP, 128), F32),
         ops=((2 * slots * KP, KP), BF16),
-        grad=((2 * n_plane * rc, 128), F32),
-        half_in=((n_plane * rc, 128), F32),
-        half=((n_plane * rc, 128), F32),
+        pot=((CH, atoms), BF16),
+        grad=((n_plane * rc, 128), F32),
         part_in=((n_plane - 1, rc, 128), F32),
         part=((rc, 128), F32),
         z_in=((n_z, rc, 128), F32),
-        pot=((CH, atoms), BF16),
-    )
-    names = tuple(args) + tuple(outs) + tuple(scratch) + ("sends", "recvs")
-    pot_all, total = call(
+    )
+    for name, value in args.items():
+        if name != "cot":
+            scratch[name] = (value.shape, value.dtype)
+    names = tuple(n + "_hbm" for n in ARGS) + tuple(outs) + tuple(scratch) + ("loads", "sends", "recvs")
+    refined, total = call(
         functools.partial(main_kernel, n_cells, n_chan, n_x, n_z, rc, names),
         list(outs.values()),
-        [pltpu.VMEM(*v) for v in scratch.values()] + [pltpu.SemaphoreType.DMA((copies,))] * 2,
-        tuple(args.values()),
+        [pltpu.VMEM(*v) for v in scratch.values()]
+        + [pltpu.SemaphoreType.DMA((n,)) for n in (len(args), copies, copies)],
+        tuple(args[n] for n in ARGS),
+        60,
+        HBM,
         collective=0,
     )
     return call(
         final_kernel,
         [shape((CH, atoms), BF16), shape((k, k, slots), F32), shape((k, k, slots), F32)],
-        [pltpu.VMEM(mix.shape, BF16)],
-        (pot_all, total, charges, mix),
+        [],
+        (refined, total),
+        60,
+        VMEM,
     )
 
 

time: 62.7 us -> 57.7 us (0.920)
  local copies, waits for them, and re-layouts: 3.49 us -> 0 us
  Pallas kernels: 58.3 us -> 56.9 us
    unnamed x5 -> x0, local copies, waits for them, and re-layouts: 3.49 us -> none
    pallas_call x2, Pallas kernels: 58.3 us -> 56.9 us  [call(): pl.pallas_call(kernel, out_shape=outs, in_specs=[space] * len(args), out_...]
where the time goes in v4:
time: 57.7 us; the launch traced here: 57.6 us
  Pallas kernels  56.9 us (99%)
  between operations  0.64 us (1%)
    pallas_call x2, Pallas kernels, call(): pl.pallas_call(kernel, out_shape=outs, in_specs=[space] * len(args), out_...  56.9 us

profile of v4, /device:TPU:1, one launch (start us, length us, event | category | flops | bytes accessed | tf_op | source)
XLA Modules:
  0.0 57.6 jit_solution(13863875719015093466)
XLA Ops:
  0.6 54.9 %shard_map.130 = (bf16[32,1024]{1,0:T(8,128)(2,1)}, f32[768,128]{1,0:T(8,128)}) custom-call(s32[1,1024]{1,0:T(1,128)} %bitcast.7, f32[25,1024]{1,0:T(8,128)} %refs_1_.1, bf16[32,1024]{1,0:T(8,128)(2,1)} %refs_2_.1, bf16[32,1024]{1,0:T(8,128)(2,1)} %refs_3_.1, bf16[25,8,25]{2,1,0:T(8,128)(2,1)} %bitcast.4, bf16[25,8,25]{2,1,0:T(8,128)(2,1)} %bitcast.5, ...), custom_call_target="tpu_custom_call" | custom-call | tf_op jit(solution)/shard_map/pallas_call | solution.py:389
  55.6 2.0 %shard_map.131 = (bf16[32,1024]{1,0:T(8,128)(2,1)}, f32[25,25,64]{2,1,0:T(8,128)}, f32[25,25,64]{2,1,0:T(8,128)}) custom-call(bf16[32,1024]{1,0:T(8,128)(2,1)} %get-tuple-element.5.refined_ref, f32[768,128]{1,0:T(8,128)} %get-tuple-element.6.total_ref), custom_call_target="tpu_custom_call" | custom-call | tf_op jit(solution)/shard_map/pallas_call | solution.py:389

commit v5 on v4

--- a/solution.py
+++ b/solution.py
@@ -136,13 +136,17 @@
     right = (lax.rem(cells + 1, n_cells), chan)
     chan_peers = [(cells, lax.rem(chan + i, n_chan)) for i in range(1, n_chan)]
     plane_peers, z_peers = [], []
-    for i in range(1, n_plane):
+    far_first = sorted(
+        range(1, n_plane),
+        key=lambda i: -min(i // (2 * n_chan), n_x - i // (2 * n_chan)) - min(i // 2 % n_chan, n_chan - i // 2 % n_chan),
+    )
+    for i in far_first:
         d = lax.rem(m + i, n_plane)
         place = d // 2
         plane_peers.append(
             (d, ((z * n_x + place // n_chan) * 2 + lax.rem(d, 2), lax.rem(place, n_chan)))
         )
-    for i in range(1, n_z):
+    for i in sorted(range(1, n_z), key=lambda i: -min(i, n_z - i)):
         d = lax.rem(z + i, n_z)
         z_peers.append((d, ((d * n_x + x) * 2 + core, chan)))
 
@@ -224,8 +228,6 @@
     c8 = (lane_iota(n_slots, 128) >> 4) * CD
     r["clists"][...] = jnp.where(at < 0, -1, jnp.where(at < CD, c8 + at, 112 + c8 + at))
 
-    turn_ops(r["leaf_ops"], r["coarse_ops"], r["ops_rows"], r["ops_turned"], r["ops"])
-    r["mixt"][...] = r["mix"][...].astype(F32).T.astype(BF16)
 
     for copy in halo:
         copy.wait()
@@ -280,20 +282,20 @@
     lax.fori_loop(0, 2, leaf_gradient, 0)
     lax.fori_loop(2, groups, leaf_group, 0)
 
-    grad, part_in, z_in, total = r["grad"], r["part_in"], r["z_in"], r["total"]
+    grad, grad16, part_in, z_in, total = (r[n] for n in ("grad", "grad16", "part_in", "z_in", "total"))
     used = k * k // 8 * 8
     grad[used:, :] = jnp.zeros((n_plane * rc - used, 128), F32)
     for j in range(k):
         turned = slots[pl.ds(j, 2 * n_slots, stride=KP), :].T
         grad[pl.ds(j, k, stride=k), :] = turned[0:k, :]
-
-    def chunk(d):
-        return pl.ds(pl.multiple_of(d * rc, 8), rc)
-
+    for d in range(n_plane):
+        grad16[d] = grad[d * rc : (d + 1) * rc, :].astype(BF16)
     plane_copies = [
-        send(grad.at[chunk(d), :], part_in.at[i], device) for i, (d, device) in enumerate(plane_peers)
+        send(grad16.at[d], part_in.at[i], device) for i, (d, device) in enumerate(plane_peers)
     ]
 
+    turn_ops(r["leaf_ops"], r["coarse_ops"], r["ops_rows"], r["ops_turned"], r["ops"])
+    r["mixt"][...] = r["mix"][...].astype(F32).T.astype(BF16)
     near = r["near"]
     far16 = dot(r["ops"][groups * SG * KP : 2 * groups * SG * KP, :], cpicked[...], TN).astype(BF16)
 
@@ -317,16 +319,16 @@
             near[:, c : c + 512] += dot(ops, picked[group_rows(g), c : c + 512], TN)
         return carry
 
-    lax.fori_loop(0, 6, near_group, 0)
+    lax.fori_loop(0, groups // 2, near_group, 0)
     for copy in plane_copies:
         copy.wait()
-    summed = grad[chunk(m), :]
+    summed = grad[pl.ds(pl.multiple_of(m * rc, 8), rc), :]
     for i in range(n_plane - 1):
-        summed = summed + part_in[i]
-    r["part"][...] = summed
+        summed = summed + part_in[i].astype(F32)
+    r["part"][...] = summed.astype(BF16)
     z_copies = [send(r["part"], z_in.at[z], device) for _, device in z_peers]
-    z_in[z] = summed
-    lax.fori_loop(6, groups, near_group, 0)
+    z_in[z] = summed.astype(BF16)
+    lax.fori_loop(groups // 2, groups, near_group, 0)
 
     expand = bexp
     for c in range(CH):
@@ -354,11 +356,11 @@
 
     for copy in z_copies:
         copy.wait()
-    summed = z_in[0]
+    summed = z_in[0].astype(F32)
     for i in range(1, n_z):
-        summed = summed + z_in[i]
-    total[chunk(m), :] = summed
-    gather_copies = [send(total.at[chunk(m), :], total.at[chunk(m), :], device) for _, device in plane_peers]
+        summed = summed + z_in[i].astype(F32)
+    total[m] = summed.astype(BF16)
+    gather_copies = [send(total.at[m], total.at[m], device) for _, device in plane_peers]
 
     for copy in pot_copies:
         copy.wait()
@@ -369,11 +371,14 @@
         copy.wait()
 
 
-def final_kernel(refined_ref, total_ref, out_ref, gl_ref, gc_ref):
+def final_kernel(refined_ref, total_ref, out_ref, gl_ref, gc_ref, rows):
     k, _, slots = gl_ref.shape
     out_ref[...] = refined_ref[...]
+    n, rc, _ = total_ref.shape
+    for d in range(n):
+        rows[d * rc : (d + 1) * rc, :] = total_ref[d].astype(F32)
     for i in range(k):
-        block = total_ref[i * k : (i + 1) * k, :]
+        block = rows[i * k : (i + 1) * k, :]
         gl_ref[i] = block[:, 0:slots]
         gc_ref[i] = pltpu.roll(block, 128 - slots, 1)[:, 0:slots]
 
@@ -410,7 +415,7 @@
     )
     outs = dict(
         refined=shape((CH, atoms), BF16),
-        total=shape((n_plane * rc, 128), F32),
+        total=shape((n_plane, rc, 128), BF16),
     )
     copies = 2 * (n_chan - 1) + 4 + 2 * (n_plane - 1) + n_z - 1
     scratch = dict(
@@ -450,9 +455,10 @@
         ops=((2 * slots * KP, KP), BF16),
         pot=((CH, atoms), BF16),
         grad=((n_plane * rc, 128), F32),
-        part_in=((n_plane - 1, rc, 128), F32),
-        part=((rc, 128), F32),
-        z_in=((n_z, rc, 128), F32),
+        grad16=((n_plane, rc, 128), BF16),
+        part_in=((n_plane - 1, rc, 128), BF16),
+        part=((rc, 128), BF16),
+        z_in=((n_z, rc, 128), BF16),
     )
     for name, value in args.items():
         if name != "cot":
@@ -471,7 +477,7 @@
     return call(
         final_kernel,
         [shape((CH, atoms), BF16), shape((k, k, slots), F32), shape((k, k, slots), F32)],
-        [],
+        [pltpu.VMEM((n_plane * rc, 128), F32)],
         (refined, total),
         60,
         VMEM,

time: 57.7 us -> 53.8 us (0.932)
  Pallas kernels: 56.9 us -> 53.1 us
    pallas_call x2, Pallas kernels: 56.9 us -> 53.1 us  [call(): pl.pallas_call(kernel, out_shape=outs, in_specs=[space] * len(args), out_...]
where the time goes in v5:
time: 53.8 us; the launch traced here: 53.7 us
  Pallas kernels  53.1 us (99%)
  between operations  0.64 us (1%)
    pallas_call x2, Pallas kernels, call(): pl.pallas_call(kernel, out_shape=outs, in_specs=[space] * len(args), out_...  53.1 us

profile of v5, /device:TPU:1, one launch (start us, length us, event | category | flops | bytes accessed | tf_op | source)
XLA Modules:
  0.0 53.7 jit_solution(17956775591901921099)
XLA Ops:
  0.6 51.1 %shard_map.130 = (bf16[32,1024]{1,0:T(8,128)(2,1)}, bf16[32,24,128]{2,1,0:T(8,128)(2,1)}) custom-call(s32[1,1024]{1,0:T(1,128)} %bitcast.7, f32[25,1024]{1,0:T(8,128)} %refs_1_.1, bf16[32,1024]{1,0:T(8,128)(2,1)} %refs_2_.1, bf16[32,1024]{1,0:T(8,128)(2,1)} %refs_3_.1, bf16[25,8,25]{2,1,0:T(8,128)(2,1)} %bitcast.4, bf16[25,8,25]{2,1,0:T(8,128)(2,1)} %bitcast.5, ...), custom_call_target="tpu_custom_call" | custom-call | tf_op jit(solution)/shard_map/pallas_call | solution.py:394
  51.8 1.9 %shard_map.131 = (bf16[32,1024]{1,0:T(8,128)(2,1)}, f32[25,25,64]{2,1,0:T(8,128)}, f32[25,25,64]{2,1,0:T(8,128)}) custom-call(bf16[32,1024]{1,0:T(8,128)(2,1)} %get-tuple-element.5.refined_ref, bf16[32,24,128]{2,1,0:T(8,128)(2,1)} %get-tuple-element.6.total_ref), custom_call_target="tpu_custom_call" | custom-call | tf_op jit(solution)/shard_map/pallas_call | solution.py:394

commit v6 on v5

--- a/solution.py
+++ b/solution.py
@@ -188,10 +188,6 @@
     load("leaf", "basis")
     fill_member(r["leaf"], member, cells * LD)
     fill_basis(r["basis"], basis_pad)
-    pl.semaphore_wait(barrier, len(greeted))
-
-    mine = pl.ds(pl.multiple_of(chan * CH, CH), CH)
-    cot_copies = [send(r["cot_hbm"], r["cot_all"].at[mine, :], d) for d in chan_peers]
 
     load("charges")
     spread(r["charges"], basis_pad, member, src)
@@ -200,7 +196,11 @@
     bottom = pltpu.roll(src[512:1024, 0:LD].astype(F32), 64, 1)
     r["to_left"][...] = jnp.where(low, top, bottom).astype(BF16)
     r["to_right"][...] = jnp.where(low, bottom, top).astype(BF16)
+
+    pl.semaphore_wait(barrier, len(greeted))
+    mine = pl.ds(pl.multiple_of(chan * CH, CH), CH)
     halo = [send(r["to_left"], r["from_right"], left), send(r["to_right"], r["from_left"], right)]
+    cot_copies = [send(r["cot_hbm"], r["cot_all"].at[mine, :], d) for d in chan_peers]
 
     load("up", "down")
     for ops_ref, pad, rows in ((r["up"], r["up_pad"], r["up_rows"]), (r["down"], r["down_pad"], r["down_rows"])):
@@ -359,15 +359,19 @@
     summed = z_in[0].astype(F32)
     for i in range(1, n_z):
         summed = summed + z_in[i].astype(F32)
-    total[m] = summed.astype(BF16)
-    gather_copies = [send(total.at[m], total.at[m], device) for _, device in plane_peers]
+    r["own"][...] = summed.astype(BF16)
+    gather_copies = [send(r["own"], total.at[m], device) for _, device in plane_peers]
+    stores = [pltpu.make_async_copy(r["own"], total.at[m], r["stores"].at[0])]
+    stores[0].start()
 
     for copy in pot_copies:
         copy.wait()
-    r["refined"][...] = (
+    r["mixed"][...] = (
         r["charges"][...].astype(F32) + dot(r["mixt"][mine, :], pot_all[...])
     ).astype(BF16)
-    for copy in gather_copies:
+    stores.append(pltpu.make_async_copy(r["mixed"], r["refined"], r["stores"].at[1]))
+    stores[1].start()
+    for copy in gather_copies + stores:
         copy.wait()
 
 
@@ -387,7 +391,7 @@
 HBM = pl.BlockSpec(memory_space=pltpu.HBM)
 
 
-def call(kernel, outs, scratch, args, mib, space, collective=None):
+def call(kernel, outs, scratch, args, kib, space, collective=None):
     extra = {}
     if collective is not None:
         extra = dict(collective_id=collective, has_side_effects=True)
@@ -395,9 +399,9 @@
         kernel,
         out_shape=outs,
         in_specs=[space] * len(args),
-        out_specs=[VMEM] * len(outs),
+        out_specs=[space if collective is not None else VMEM] * len(outs),
         scratch_shapes=scratch,
-        compiler_params=pltpu.CompilerParams(vmem_limit_bytes=mib << 20, **extra),
+        compiler_params=pltpu.CompilerParams(vmem_limit_bytes=kib << 10, **extra),
     )(*args)
 
 
@@ -458,19 +462,21 @@
         grad16=((n_plane, rc, 128), BF16),
         part_in=((n_plane - 1, rc, 128), BF16),
         part=((rc, 128), BF16),
+        own=((rc, 128), BF16),
+        mixed=((CH, atoms), BF16),
         z_in=((n_z, rc, 128), BF16),
     )
     for name, value in args.items():
         if name != "cot":
             scratch[name] = (value.shape, value.dtype)
-    names = tuple(n + "_hbm" for n in ARGS) + tuple(outs) + tuple(scratch) + ("loads", "sends", "recvs")
+    names = tuple(n + "_hbm" for n in ARGS) + tuple(outs) + tuple(scratch) + ("loads", "stores", "sends", "recvs")
     refined, total = call(
         functools.partial(main_kernel, n_cells, n_chan, n_x, n_z, rc, names),
         list(outs.values()),
         [pltpu.VMEM(*v) for v in scratch.values()]
-        + [pltpu.SemaphoreType.DMA((n,)) for n in (len(args), copies, copies)],
+        + [pltpu.SemaphoreType.DMA((n,)) for n in (len(args), 2, copies, copies)],
         tuple(args[n] for n in ARGS),
-        60,
+        60 << 10,
         HBM,
         collective=0,
     )
@@ -479,7 +485,7 @@
         [shape((CH, atoms), BF16), shape((k, k, slots), F32), shape((k, k, slots), F32)],
         [pltpu.VMEM((n_plane * rc, 128), F32)],
         (refined, total),
-        60,
+        60 << 10,
         VMEM,
     )
 

time: 53.8 us -> 52.2 us (0.970)
  Pallas kernels: 53.1 us -> 51.5 us
    pallas_call x2, Pallas kernels: 53.1 us -> 51.5 us  [call(): pl.pallas_call(kernel, out_shape=outs, in_specs=[space] * len(args), out_...]
where the time goes in v6:
time: 52.2 us; the launch traced here: 52.1 us
  Pallas kernels  51.5 us (99%)
  between operations  0.64 us (1%)
    pallas_call x2, Pallas kernels, call(): pl.pallas_call(kernel, out_shape=outs, in_specs=[space] * len(args), out_...  51.5 us

profile of v6, /device:TPU:1, one launch (start us, length us, event | category | flops | bytes accessed | tf_op | source)
XLA Modules:
  0.0 52.1 jit_solution(12681881256626665427)
XLA Ops:
  0.6 49.5 %shard_map.130 = (bf16[32,1024]{1,0:T(8,128)(2,1)}, bf16[32,24,128]{2,1,0:T(8,128)(2,1)}) custom-call(s32[1,1024]{1,0:T(1,128)} %bitcast.7, f32[25,1024]{1,0:T(8,128)} %refs_1_.1, bf16[32,1024]{1,0:T(8,128)(2,1)} %refs_2_.1, bf16[32,1024]{1,0:T(8,128)(2,1)} %refs_3_.1, bf16[25,8,25]{2,1,0:T(8,128)(2,1)} %bitcast.4, bf16[25,8,25]{2,1,0:T(8,128)(2,1)} %bitcast.5, ...), custom_call_target="tpu_custom_call" | custom-call | tf_op jit(solution)/shard_map/pallas_call | solution.py:398
  50.2 1.9 %shard_map.131 = (bf16[32,1024]{1,0:T(8,128)(2,1)}, f32[25,25,64]{2,1,0:T(8,128)}, f32[25,25,64]{2,1,0:T(8,128)}) custom-call(bf16[32,1024]{1,0:T(8,128)(2,1)} %get-tuple-element.5.refined_ref, bf16[32,24,128]{2,1,0:T(8,128)(2,1)} %get-tuple-element.6.total_ref), custom_call_target="tpu_custom_call" | custom-call | tf_op jit(solution)/shard_map/pallas_call | solution.py:398

commit v7 on v6

--- a/solution.py
+++ b/solution.py
@@ -134,7 +134,9 @@
     groups = n_slots // SG
     left = (lax.rem(cells + n_cells - 1, n_cells), chan)
     right = (lax.rem(cells + 1, n_cells), chan)
-    chan_peers = [(cells, lax.rem(chan + i, n_chan)) for i in range(1, n_chan)]
+    chan_peers = [
+        (cells, lax.rem(chan + i, n_chan)) for i in sorted(range(1, n_chan), key=lambda i: -min(i, n_chan - i))
+    ]
     plane_peers, z_peers = [], []
     far_first = sorted(
         range(1, n_plane),
@@ -246,14 +248,6 @@
 
     lax.fori_loop(0, 2, leaf_gather, 0)
 
-    for copy in cot_copies:
-        copy.wait()
-    r["back_pot"][...] = dot(r["mix"][mine, :], r["cot_all"][...]).astype(BF16)
-    spread(r["back_pot"], basis_pad, member, bexp)
-    for c in range(CH):
-        r["back"][:, c * LD : (c + 1) * LD] = bexp[c * KP : (c + 1) * KP, :]
-    r["bfar"][...] = to_parents(bexp, r["octants"], down_tall, TN, r["stack"])
-
     for copy in coarse_halo:
         copy.wait()
     first = (lane_iota(KP, 128) & 15) < 8
@@ -273,6 +267,15 @@
         return carry
 
     lax.fori_loop(0, groups // 2, coarse_group, 0)
+
+    for copy in cot_copies:
+        copy.wait()
+    r["back_pot"][...] = dot(r["mix"][mine, :], r["cot_all"][...]).astype(BF16)
+    spread(r["back_pot"], basis_pad, member, bexp)
+    for c in range(CH):
+        r["back"][:, c * LD : (c + 1) * LD] = bexp[c * KP : (c + 1) * KP, :]
+    r["bfar"][...] = to_parents(bexp, r["octants"], down_tall, TN, r["stack"])
+
     slots[groups * SG * KP : 2 * groups * SG * KP, 0:KP] = dot(cpicked[...], r["bfar"][...], NT)
 
     def leaf_group(g, carry):

time: 52.2 us -> 52.1 us (level)
  no operation moved by 1% of the time
where the time goes in v7:
time: 52.1 us; the launch traced here: 52 us
  Pallas kernels  51.4 us (99%)
  between operations  0.64 us (1%)
    pallas_call x2, Pallas kernels, call(): pl.pallas_call(kernel, out_shape=outs, in_specs=[space] * len(args), out_...  51.4 us

profile of v7, /device:TPU:1, one launch (start us, length us, event | category | flops | bytes accessed | tf_op | source)
XLA Modules:
  0.0 52.0 jit_solution(303825107050237982)
XLA Ops:
  0.6 49.4 %shard_map.130 = (bf16[32,1024]{1,0:T(8,128)(2,1)}, bf16[32,24,128]{2,1,0:T(8,128)(2,1)}) custom-call(s32[1,1024]{1,0:T(1,128)} %bitcast.7, f32[25,1024]{1,0:T(8,128)} %refs_1_.1, bf16[32,1024]{1,0:T(8,128)(2,1)} %refs_2_.1, bf16[32,1024]{1,0:T(8,128)(2,1)} %refs_3_.1, bf16[25,8,25]{2,1,0:T(8,128)(2,1)} %bitcast.4, bf16[25,8,25]{2,1,0:T(8,128)(2,1)} %bitcast.5, ...), custom_call_target="tpu_custom_call" | custom-call | tf_op jit(solution)/shard_map/pallas_call | solution.py:401
  50.1 1.9 %shard_map.131 = (bf16[32,1024]{1,0:T(8,128)(2,1)}, f32[25,25,64]{2,1,0:T(8,128)}, f32[25,25,64]{2,1,0:T(8,128)}) custom-call(bf16[32,1024]{1,0:T(8,128)(2,1)} %get-tuple-element.5.refined_ref, bf16[32,24,128]{2,1,0:T(8,128)(2,1)} %get-tuple-element.6.total_ref), custom_call_target="tpu_custom_call" | custom-call | tf_op jit(solution)/shard_map/pallas_call | solution.py:401

commit v8 on v6

--- a/solution.py
+++ b/solution.py
@@ -197,6 +197,7 @@
     r["to_left"][...] = jnp.where(low, top, bottom).astype(BF16)
     r["to_right"][...] = jnp.where(low, bottom, top).astype(BF16)
 
+    fill_octants(r["octants"])
     pl.semaphore_wait(barrier, len(greeted))
     mine = pl.ds(pl.multiple_of(chan * CH, CH), CH)
     halo = [send(r["to_left"], r["from_right"], left), send(r["to_right"], r["from_left"], right)]
@@ -209,7 +210,6 @@
             rows[i * 8 : (i + 1) * 8, 0:k] = ops_ref[i].astype(F32)
         for o in range(8):
             pad[o * KP : o * KP + k, 0:k] = rows[pl.ds(o, k, stride=8), :][:, 0:k]
-    fill_octants(r["octants"])
 
     up_wide = jnp.concatenate([r["up_pad"][o * KP : (o + 1) * KP, :] for o in range(8)], axis=1).astype(BF16)
     down_wide = jnp.concatenate([r["down_pad"][o * KP : (o + 1) * KP, :] for o in range(8)], axis=1).astype(BF16)

time: 52.2 us -> 52.8 us (1.011)
    pallas_call x2, Pallas kernels: 51.5 us -> 52 us  [call(): pl.pallas_call(kernel, out_shape=outs, in_specs=[space] * len(args), out_...]
where the time goes in v8:
time: 52.8 us; the launch traced here: 52.7 us
  Pallas kernels  52 us (98%)
  between operations  0.64 us (1%)
    pallas_call x2, Pallas kernels, call(): pl.pallas_call(kernel, out_shape=outs, in_specs=[space] * len(args), out_...  52 us

profile of v8, /device:TPU:1, one launch (start us, length us, event | category | flops | bytes accessed | tf_op | source)
XLA Modules:
  0.0 52.7 jit_solution(11094747305887938407)
XLA Ops:
  0.6 50.1 %shard_map.130 = (bf16[32,1024]{1,0:T(8,128)(2,1)}, bf16[32,24,128]{2,1,0:T(8,128)(2,1)}) custom-call(s32[1,1024]{1,0:T(1,128)} %bitcast.7, f32[25,1024]{1,0:T(8,128)} %refs_1_.1, bf16[32,1024]{1,0:T(8,128)(2,1)} %refs_2_.1, bf16[32,1024]{1,0:T(8,128)(2,1)} %refs_3_.1, bf16[25,8,25]{2,1,0:T(8,128)(2,1)} %bitcast.4, bf16[25,8,25]{2,1,0:T(8,128)(2,1)} %bitcast.5, ...), custom_call_target="tpu_custom_call" | custom-call | tf_op jit(solution)/shard_map/pallas_call | solution.py:398
  50.7 1.9 %shard_map.131 = (bf16[32,1024]{1,0:T(8,128)(2,1)}, f32[25,25,64]{2,1,0:T(8,128)}, f32[25,25,64]{2,1,0:T(8,128)}) custom-call(bf16[32,1024]{1,0:T(8,128)(2,1)} %get-tuple-element.5.refined_ref, bf16[32,24,128]{2,1,0:T(8,128)(2,1)} %get-tuple-element.6.total_ref), custom_call_target="tpu_custom_call" | custom-call | tf_op jit(solution)/shard_map/pallas_call | solution.py:398
